TPU v7x, 32 devices: a whole 2x2x4 slice. The times are simulated.
32 devices in a mesh: dp: 16 (over z, y, x), tensor: 2 (over core).
Axes of the slice: x: 2, y: 2, z: 4, core: 2. Of those that a mesh axis runs over, the one named last changes fastest.
Arguments:
- layer_input: bfloat16 [16, 1024, 1024], P('dp', 'tensor'), may hold values from -6 to 6
- memory: bfloat16 [16, 512, 1024], P('dp', 'tensor'), may hold values from -6 to 6
- evicted: bfloat16 [16, 1536, 1024], P('dp', 'tensor'), may hold values from -6 to 6
- picture_start: int32 [16], P('dp'), may hold values from 0 to 768, as said below
- memory_lengths: int32 [16, 2], P('dp'), may hold values from 128 to 512, as said below
- w_query: bfloat16 [1024, 1024], P('dp', 'tensor'), may hold values from -0.1875 to 0.1875
- w_key: bfloat16 [1024, 1024], P('dp', 'tensor'), may hold values from -0.1875 to 0.1875
- w_value: bfloat16 [1024, 1024], P('dp', 'tensor'), may hold values from -0.1875 to 0.1875
- w_output: bfloat16 [1024, 1024], P('tensor', 'dp'), may hold values from -1.5 to 1.5
- w_compress: bfloat16 [3072, 1024], P(('dp', 'tensor')), may hold values from -0.109375 to 0.109375
- gain_attn: bfloat16 [1024], P(('dp', 'tensor')), may hold values from 0.5 to 1.5
- gain_ffn: bfloat16 [1024], P(('dp', 'tensor')), may hold values from 0.5 to 1.5
- w_inner: bfloat16 [1024, 4096], P('dp', 'tensor'), may hold values from -0.1875 to 0.1875
- w_outer: bfloat16 [4096, 1024], P('tensor', 'dp'), may hold values from -0.09375 to 0.09375
- cotangent: bfloat16 [16, 1024, 1024], P('dp', 'tensor'), may hold values from -6 to 6
Outputs:
- layer_output: bfloat16 [16, 1024, 1024], P('dp', 'tensor')
- input_grad: bfloat16 [16, 1024, 1024], P('dp', 'tensor')
- grad_query: float32 [1024, 1024], P('dp', 'tensor')
- grad_key: float32 [1024, 1024], P('dp', 'tensor')
- grad_value: float32 [1024, 1024], P('dp', 'tensor')
- grad_output_proj: float32 [1024, 1024], P('tensor', 'dp')
- grad_compress: float32 [3072, 1024], P(('dp', 'tensor'))
- grad_gain_attn: float32 [1024], P(('dp', 'tensor'))
- grad_gain_ffn: float32 [1024], P(('dp', 'tensor'))
- grad_inner: float32 [1024, 4096], P('dp', 'tensor')
- grad_outer: float32 [4096, 1024], P('tensor', 'dp')
- branch_rms: float32 [16, 3], P('dp')
Inputs may be any that keep to these rules, and one draw needn't show every extreme that they name: Sequence s treats tokens picture_start[s] to picture_start[s] + 255 as one picture span; starts are multiples of half of 256. `memory_lengths`: column 0 counts the valid most recent rows of memory, column 1 those of compressed memory.
All inputs are finite; a program needn't handle non-finite values.
Results may differ from a plain program's by a relative error of at most 0.018.
Values may be sent and summed in bfloat16 or wider, within the bound.
No kernel may reach another device: no remote copies, remote signals or barrier semaphores. Data moves between devices by JAX's collectives and lax.ppermute only.
A program may use at most 256 MiB of HBM per device.

v0:
```python
import jax
import jax.numpy as jnp
from jax import lax
from jax.experimental import pallas as pl
from jax.experimental.pallas import tpu as pltpu
from jax.sharding import PartitionSpec as P


D = 1024
DH = 128
MEM = 512
CMEM = 512
PIC = 256
L = 1024

epsilon = 1e-06
very_negative = -1e30


F32 = jnp.float32
BF16 = jnp.bfloat16
AXES = ("dp", "tensor")


def matmul(a, b, dims, out=F32):
    return lax.dot_general(a, b, (dims, ((), ())), preferred_element_type=F32).astype(out)


def nn(a, b, out=F32):
    return matmul(a, b, ((1,), (0,)), out)


def nt(a, b, out=F32):
    return matmul(a, b, ((1,), (1,)), out)


def tn(a, b, out=F32):
    return matmul(a, b, ((0,), (0,)), out)


class Cube:
    def __init__(self, n, cores):
        self.n, self.cores = n, cores
        self.far = n // 4
        self.low = [(1, 0) if c % 2 == 0 else (0, 1) for c in range(cores)]
        self.masks = [
            [
                (j % self.far) * 4
                + ((j // self.far) & 1) * (1 << first)
                + (j // (2 * self.far)) * (1 << second)
                for j in range(n)
            ]
            for first, second in self.low
        ]
        self.dp = lax.axis_index("dp")
        self.core = lax.axis_index("tensor")
        table = jnp.array(self.masks, jnp.int32)
        self.own = lax.dynamic_index_in_dim(table, self.core, 0, keepdims=False) ^ self.dp

    def send(self, value, flips):
        pairs = [
            (d * self.cores + c, (d ^ flips[c]) * self.cores + c)
            for d in range(self.n)
            for c in range(self.cores)
        ]
        return lax.ppermute(value, AXES, pairs)

    def far_send(self, value, m):
        return self.send(value, [4 * m] * self.cores)

    def low_swap(self, value, which):
        return self.send(value, [1 << pair[which] for pair in self.low])

    def core_swap(self, value):
        return lax.ppermute(value, "tensor", [(0, 1), (1, 0)])

    def reduce(self, low, high):
        arrived = self.low_swap(high, 1)
        half = low.shape[0] // 2

        def added(part, other, run):
            return part[run].astype(F32) + other[run].astype(F32)

        far = slice(half, None)
        near = added(low, arrived, slice(0, half))
        far_sum = added(low, arrived, far).astype(BF16)
        arrived = self.low_swap(far_sum, 0)
        total = near[0] + arrived[0].astype(F32)
        sent = [
            self.far_send(added(near, arrived, slice(m, m + 1)).astype(BF16), m)
            for m in range(1, self.far)
        ]
        for block in sent:
            total = total + block[0].astype(F32)
        return total


ANY = pl.BlockSpec(memory_space=pl.ANY)
SMEM = pl.BlockSpec(memory_space=pltpu.SMEM)
VMEM = pl.BlockSpec(memory_space=pltpu.VMEM)


def run_copies(copies):
    for copy in copies:
        copy.start()
    for copy in copies:
        copy.wait()


def place(parts, where, pieces, outs):
    rows = parts[0].shape[1]
    count = where.shape[0]

    def body(where_ref, *refs):
        ins, out_refs, sem = refs[: len(parts)], refs[len(parts) : -1], refs[-1]
        copies, j = [], 0
        for source in ins:
            for b in range(source.shape[0]):
                at = 0
                for i, (width, out, row) in enumerate(pieces):
                    copies.append(
                        pltpu.make_async_copy(
                            source.at[b, :, pl.ds(at, width)],
                            out_refs[out].at[where_ref[j], pl.ds(row, rows)],
                            sem.at[j * len(pieces) + i],
                        )
                    )
                    at += width
                j += 1
        run_copies(copies)

    filled = pl.pallas_call(
        body,
        out_shape=[jax.ShapeDtypeStruct((count, r, w), parts[0].dtype) for r, w in outs],
        in_specs=[SMEM] + [ANY] * len(parts),
        out_specs=[VMEM] * len(outs),
        scratch_shapes=[pltpu.SemaphoreType.DMA((count * len(pieces),))],
        name="place",
    )(where, *parts)
    return [o.reshape(count * r, w) for o, (r, w) in zip(filled, outs)]


def pick(blocks, where, below=None):
    count = where.shape[0]
    rows = blocks[0].shape[1]
    width = sum(b.shape[2] for b in blocks)
    half = count // 2
    ins = list(blocks) + ([] if below is None else [below])
    total = rows + (0 if below is None else below.shape[1])

    def body(where_ref, *refs):
        sources, (low, high, sem) = refs[: len(ins)], refs[len(ins) :]
        copies = []
        for j in range(count):
            at = 0
            out = (low if j < half else high).at[j % half]
            for i, source in enumerate(sources):
                if i < len(blocks):
                    target = out.at[pl.ds(0, rows), pl.ds(at, source.shape[2])]
                    at += source.shape[2]
                else:
                    target = out.at[pl.ds(rows, source.shape[1])]
                copies.append(
                    pltpu.make_async_copy(
                        source.at[where_ref[j]], target, sem.at[j * len(ins) + i]
                    )
                )
        run_copies(copies)

    return pl.pallas_call(
        body,
        out_shape=[jax.ShapeDtypeStruct((half, total, width), BF16)] * 2,
        in_specs=[SMEM] + [ANY] * len(ins),
        out_specs=[VMEM] * 2,
        scratch_shapes=[pltpu.SemaphoreType.DMA((count * len(ins),))],
        name="pick",
    )(where, *ins)


def rms_norm(matrix_rows, gain_vec):
    return (
        matrix_rows
        * lax.rsqrt(jnp.mean(matrix_rows * matrix_rows, axis=-1, keepdims=True) + epsilon)
        * gain_vec
    )


def gelu_tanh(inner_in):
    return jax.nn.gelu(inner_in, approximate=True)


LOG2E = 1.4426950408889634


def key_runs(core, half, kind, part_rows, comp_part, mem_part):
    base = jnp.bitwise_xor(core, half) * part_rows
    offset = {"comp": 0, "mem": comp_part, "tok": comp_part + mem_part}[kind]
    return pl.multiple_of(base + offset, 128)


def attention_chunks(info, q_half, shapes):
    comp_part, mem_part, tok_part = shapes
    part_rows = comp_part + mem_part + tok_part
    core, span, mem_len, comp_len = info[0], info[1], info[2], info[3]

    def start(kind, half):
        return key_runs(core, half, kind, part_rows, comp_part, mem_part)

    def tail(first, total, length):
        def masker(shape):
            row = lax.broadcasted_iota(jnp.int32, shape, 0) + first
            return row >= total - length

        return masker

    def causal(half):
        def masker(shape):
            key = lax.broadcasted_iota(jnp.int32, shape, 0) + half * tok_part
            query = lax.broadcasted_iota(jnp.int32, shape, 1) + q_half * tok_part
            key_in = (key >= span) & (key < span + PIC)
            query_in = (query >= span) & (query < span + PIC)
            return (key <= query) | (key_in & query_in)

        return masker

    chunks = []
    for half in (0, 1):
        chunks.append((start("comp", half), comp_part, tail(half * comp_part, CMEM, comp_len), None))
    for half in (0, 1):
        chunks.append((start("mem", half), mem_part, tail(half * mem_part, MEM, mem_len), None))
    crosses = (span < tok_part) & (span + PIC > tok_part)
    chunks.append((start("tok", 0), tok_part, None, q_half == 1))
    chunks.append((start("tok", 0), tok_part, causal(0), q_half == 0))
    chunks.append((start("tok", 1), tok_part, causal(1), (q_half == 1) | crosses))
    return chunks


def attend(info, query_rows, keyval, shapes, heads):
    rows = keyval.shape[0]
    q_part = query_rows.shape[0] // 2
    factor = DH ** (-0.5) * LOG2E

    def body(info_ref, q_ref, kv_ref, o_ref, lse_ref, vt_ref, m_ref, l_ref, acc_ref):
        q_half = pl.program_id(1)

        @pl.when(q_half == 0)
        def _():
            vt_ref[...] = kv_ref[:, DH:].T

        m_ref[...] = jnp.full_like(m_ref, very_negative)
        l_ref[...] = jnp.zeros_like(l_ref)
        acc_ref[...] = jnp.zeros_like(acc_ref)
        q = q_ref[...]
        for first, count, masker, needed in attention_chunks(info_ref, q_half, shapes):

            def step(first=first, count=count, masker=masker):
                s = nt(kv_ref[pl.ds(first, count), :DH], q)
                if masker is not None:
                    s = jnp.where(masker(s.shape), s, very_negative)
                m_old = m_ref[...]
                m_new = jnp.maximum(m_old, jnp.max(s, axis=0, keepdims=True))
                shrink = jnp.exp2((m_old - m_new) * factor)
                p = jnp.exp2((s - m_new) * factor)
                l_ref[...] = l_ref[...] * shrink + jnp.sum(p, axis=0, keepdims=True)
                acc_ref[...] = acc_ref[...] * shrink + nn(
                    vt_ref[:, pl.ds(first, count)], p.astype(BF16)
                )
                m_ref[...] = m_new

            if needed is None:
                step()
            else:
                pl.when(needed)(step)
        total = l_ref[...]
        o_ref[...] = (acc_ref[...] / total).T.astype(BF16)
        lse_ref[...] = (m_ref[...] * factor + jnp.log2(total))[None]

    def q_map(h, a, info_ref):
        return (jnp.bitwise_xor(a, info_ref[0]), h)

    return pl.pallas_call(
        body,
        out_shape=(
            jax.ShapeDtypeStruct(query_rows.shape, BF16),
            jax.ShapeDtypeStruct((heads * 2, 1, q_part), F32),
        ),
        grid_spec=pltpu.PrefetchScalarGridSpec(
            num_scalar_prefetch=1,
            grid=(heads, 2),
            in_specs=[
                pl.BlockSpec((q_part, DH), q_map),
                pl.BlockSpec((rows, 2 * DH), lambda h, a, i: (0, h)),
            ],
            out_specs=[
                pl.BlockSpec((q_part, DH), q_map),
                pl.BlockSpec((1, 1, q_part), lambda h, a, i: (h * 2 + a, 0, 0)),
            ],
            scratch_shapes=[
                pltpu.VMEM((DH, rows), BF16),
                pltpu.VMEM((1, q_part), F32),
                pltpu.VMEM((1, q_part), F32),
                pltpu.VMEM((DH, q_part), F32),
            ],
        ),
        name="attend",
    )(info, query_rows, keyval)


def attend_back(info, query_rows, keyval, mixed, d_mixed, lse, shapes, skip, heads, carry=None):
    rows = keyval.shape[0]
    q_part = query_rows.shape[0] // 2
    scale = DH ** (-0.5)
    factor = scale * LOG2E

    def body(info_ref, q_ref, kv_ref, o_ref, g_ref, lse_ref, *refs):
        dq_ref, dkv_ref, kt_ref, dk_acc, dv_acc, dq_acc = refs[-6:]
        q_half = pl.program_id(1)

        @pl.when(q_half == 0)
        def _():
            kt_ref[...] = kv_ref[:, :DH].T
            dk_acc[...] = jnp.zeros_like(dk_acc)
            dv_acc[...] = jnp.zeros_like(dv_acc)

        dq_acc[...] = jnp.zeros_like(dq_acc)
        q, g = q_ref[...], g_ref[...]
        lse_row = lse_ref[0]
        delta = jnp.sum((g.astype(F32) * o_ref[...].astype(F32)).T, axis=0, keepdims=True)
        for first, count, masker, needed in attention_chunks(info_ref, q_half, shapes):

            def step(first=first, count=count, masker=masker):
                run = pl.ds(first, count)
                p = jnp.exp2(nt(kv_ref[run, :DH], q) * factor - lse_row)
                if masker is not None:
                    p = jnp.where(masker(p.shape), p, 0.0)
                d_p = nt(kv_ref[run, DH:], g)
                d_s = (p * (d_p - delta)).astype(BF16)
                dv_acc[run, :] += nn(p.astype(BF16), g)
                dk_acc[run, :] += nn(d_s, q)
                dq_acc[...] += nn(kt_ref[:, run], d_s)

            if needed is None:
                step()
            else:
                pl.when(needed)(step)
        dq_ref[...] = (dq_acc[...] * scale).T.astype(BF16)

        @pl.when(q_half == 1)
        def _():
            dkv_ref[:, :DH] = (dk_acc[...] * scale).astype(BF16)
            dkv_ref[:, DH:] = dv_acc[...].astype(BF16)

    def q_map(h, a, info_ref):
        return (jnp.bitwise_xor(a, info_ref[0]), h + skip)

    q_spec = pl.BlockSpec((q_part, DH), q_map)
    kv_spec = pl.BlockSpec((rows, 2 * DH), lambda h, a, i: (0, h + skip))
    lse_spec = pl.BlockSpec((1, 1, q_part), lambda h, a, i: ((h + skip) * 2 + a, 0, 0))
    carried = [] if carry is None else list(carry)
    return pl.pallas_call(
        body,
        out_shape=(
            jax.ShapeDtypeStruct(query_rows.shape, BF16),
            jax.ShapeDtypeStruct(keyval.shape, BF16),
        ),
        grid_spec=pltpu.PrefetchScalarGridSpec(
            num_scalar_prefetch=1,
            grid=(heads, 2),
            in_specs=[q_spec, kv_spec, q_spec, q_spec, lse_spec] + [ANY] * len(carried),
            out_specs=[q_spec, kv_spec],
            scratch_shapes=[
                pltpu.VMEM((DH, rows), BF16),
                pltpu.VMEM((rows, DH), F32),
                pltpu.VMEM((rows, DH), F32),
                pltpu.VMEM((DH, q_part), F32),
            ],
        ),
        input_output_aliases={6 + i: i for i in range(len(carried))},
        name="attend_back",
    )(info, query_rows, keyval, mixed, d_mixed, lse, *carried)


def per_device(
    layer_input,
    memory,
    evicted,
    picture_start,
    memory_lengths,
    w_query,
    w_key,
    w_value,
    w_output,
    w_compress,
    gain_attn,
    gain_ffn,
    w_inner,
    w_outer,
    cotangent,
):
    cube = Cube(lax.axis_size("dp"), lax.axis_size("tensor"))
    n, core = cube.n, cube.core
    tokens, memory, evicted, cotangent = layer_input[0], memory[0], evicted[0], cotangent[0]
    tok_part, mem_part, comp_part = tokens.shape[0], memory.shape[0], evicted.shape[0] // 3
    parts = (comp_part, mem_part, tok_part)
    width = w_query.shape[1]
    heads = width // DH
    rows = comp_part + mem_part + tok_part
    inner_width = w_inner.shape[1]
    share = gain_attn.shape[0]
    shard_rows = w_query.shape[0]

    def by_core(own, other, axis):
        flip = core > 0
        return jnp.concatenate(
            [jnp.where(flip, other, own), jnp.where(flip, own, other)], axis=axis
        )

    def gathered(shard, pieces, outs):
        held = [shard[None]] + [cube.far_send(shard[None], m) for m in range(1, cube.far)]
        held = jnp.concatenate(held, axis=0)
        arrived = cube.low_swap(held, 0)
        held = jnp.concatenate([held, arrived], axis=0)
        arrived = cube.low_swap(held, 1)
        return place([held, arrived], cube.own, pieces, outs)

    def picked(blocks, below=None):
        return pick(blocks, cube.own, below)

    col_half = D // 2
    send_cols = jnp.where(core > 0, w_compress[:, :col_half], w_compress[:, col_half:])
    keep_cols = jnp.where(core > 0, w_compress[:, col_half:], w_compress[:, :col_half])
    compress_cols = by_core(keep_cols, cube.core_swap(send_cols), 0)
    gains_own = jnp.stack([gain_attn, gain_ffn])
    gain_pair = by_core(gains_own[None], cube.core_swap(gains_own)[None], 0)
    gain_row = jnp.pad(gain_pair.reshape(1, -1), ((0, shard_rows - 1), (0, 128 - 4 * share)))
    columns = [w_query]
    for h in range(heads):
        head = slice(h * DH, (h + 1) * DH)
        columns += [w_key[:, head], w_value[:, head]]
    columns += [gain_row]
    folds = compress_cols.shape[0] // shard_rows
    columns += [compress_cols[i * shard_rows : (i + 1) * shard_rows] for i in range(folds)]
    query_w, keyval_w, gain_rows, compress_w = gathered(
        jnp.concatenate(columns, axis=1),
        [(width, 0, 0), (2 * width, 1, 0), (128, 2, 0)]
        + [(col_half, 3, i * shard_rows) for i in range(folds)],
        [
            (shard_rows, width),
            (shard_rows, 2 * width),
            (shard_rows, 128),
            (folds * shard_rows, col_half),
        ],
    )
    output_t, inner_w = gathered(
        jnp.concatenate([w_output.T, w_inner], axis=1),
        [(width, 0, 0), (inner_width, 1, 0)],
        [(shard_rows, width), (shard_rows, inner_width)],
    )
    (outer_t,) = gathered(w_outer.T, [(inner_width, 0, 0)], [(shard_rows, inner_width)])
    gains = gain_rows.reshape(n, shard_rows, 128)[:, 0, : 4 * share].reshape(n, 2, 2, share)
    gains = jnp.transpose(gains, (2, 0, 1, 3)).reshape(2, D).astype(F32)
    gain_attn_f, gain_ffn_f = gains[0], gains[1]

    info = jnp.concatenate([core[None], picture_start, memory_lengths[0]]).astype(jnp.int32)
    grouped_own = evicted.reshape(comp_part, 3 * D)
    grouped = jnp.concatenate([grouped_own, cube.core_swap(grouped_own)], axis=0)
    grouped_t = lax.optimization_barrier(grouped.T)
    comp_cols = nn(grouped, compress_w)
    compressed = by_core(comp_cols[:comp_part], cube.core_swap(comp_cols[comp_part:]), 1)
    token_f = tokens.astype(F32)
    keyed_rows = jnp.concatenate([compressed, memory.astype(F32), token_f], axis=0)
    attn_value, attn_pull = jax.vjp(rms_norm, keyed_rows, gain_attn_f)
    attn_normed = attn_value.astype(BF16)
    all_rows = jnp.concatenate([attn_normed, cube.core_swap(attn_normed)], axis=0)
    tok_at = comp_part + mem_part
    token_rows = jnp.concatenate([all_rows[tok_at:rows], all_rows[rows + tok_at :]], axis=0)
    query_rows = nn(token_rows, query_w, BF16)
    keyval = nn(all_rows, keyval_w, BF16)
    mixed, lse = attend(info, query_rows, keyval, parts, heads)

    def summed_share(full, other_side):
        away = cube.core_swap(nt(full[tok_part:], other_side, BF16))
        return nt(full[:tok_part], other_side) + away.astype(F32)

    attn_branch = summed_share(mixed, output_t)
    after_attn = token_f + attn_branch
    ffn_value, ffn_pull = jax.vjp(rms_norm, after_attn, gain_ffn_f)
    ffn_own = ffn_value.astype(BF16)
    ffn_rows = jnp.concatenate([ffn_own, cube.core_swap(ffn_own)], axis=0)
    inner_hidden = nn(ffn_rows, inner_w)
    active_f, gelu_pull = jax.vjp(gelu_tanh, inner_hidden)
    active = active_f.astype(BF16)
    ffn_branch = summed_share(active, outer_t)
    summed = after_attn + ffn_branch
    layer_output = summed.astype(BF16)
    square_sums = jnp.stack(
        [
            jnp.sum(attn_branch * attn_branch),
            jnp.sum(ffn_branch * ffn_branch),
            jnp.sum(summed * summed),
        ]
    )
    branch_rms = jnp.sqrt((square_sums + cube.core_swap(square_sums)) / (L * D))[None]

    def split(partial):
        return partial.reshape(n, partial.shape[0] // n, partial.shape[1])

    out_grads = jnp.concatenate([cotangent, cube.core_swap(cotangent)], axis=0)
    grad_outer = cube.reduce(*picked([split(tn(out_grads, active, BF16))])).T
    d_active = nn(out_grads, outer_t)
    d_inner = gelu_pull(d_active)[0].astype(BF16)
    d_ffn_normed = summed_share(d_inner, inner_w)
    d_after, d_gain_ffn = ffn_pull(d_ffn_normed)
    grad_after = cotangent.astype(F32) + d_after
    grad_after_own = grad_after.astype(BF16)
    attn_grads = jnp.concatenate([grad_after_own, cube.core_swap(grad_after_own)], axis=0)
    out_inner = cube.reduce(
        *picked([split(tn(attn_grads, mixed, BF16)), split(tn(ffn_rows, d_inner, BF16))]),
    )
    grad_output, grad_inner = out_inner[:, :width].T, out_inner[:, width:]
    d_mixed = nn(attn_grads, output_t, BF16)
    back = info, query_rows, keyval, mixed, d_mixed, lse, parts
    carry = attend_back(*back, 0, heads // 2)
    d_queries, d_keyval = attend_back(*back, heads // 2, heads - heads // 2, carry)
    near_qkv, far_qkv = picked(
        [split(tn(token_rows, d_queries, BF16)), split(tn(all_rows, d_keyval, BF16))]
    )
    qkv = cube.reduce(near_qkv, far_qkv)
    d_queries, d_keyval = lax.optimization_barrier((d_queries, d_keyval, near_qkv, far_qkv))[:2]
    grad_query = qkv[:, :width]
    key_cols = [qkv[:, width + 2 * h * DH :][:, :DH] for h in range(heads)]
    value_cols = [qkv[:, width + (2 * h + 1) * DH :][:, :DH] for h in range(heads)]
    grad_key = jnp.concatenate(key_cols, axis=1)
    grad_value = jnp.concatenate(value_cols, axis=1)
    d_rows = nt(d_keyval, keyval_w)
    d_tok = nt(d_queries, query_w)
    d_own = jnp.concatenate([d_rows[:tok_at], d_rows[tok_at:rows] + d_tok[:tok_part]], axis=0)
    d_other = jnp.concatenate(
        [d_rows[rows : rows + tok_at], d_rows[rows + tok_at :] + d_tok[tok_part:]], axis=0
    ).astype(BF16)
    d_attn_normed = d_own + cube.core_swap(d_other).astype(F32)
    d_keyed, d_gain_attn = attn_pull(d_attn_normed)
    input_grad = (grad_after + d_keyed[tok_at:]).astype(BF16)
    d_comp = d_keyed[:comp_part].astype(BF16)
    d_send = jnp.where(core > 0, d_comp[:, :col_half], d_comp[:, col_half:])
    d_keep = jnp.where(core > 0, d_comp[:, col_half:], d_comp[:, :col_half])
    d_comp_cols = jnp.concatenate([d_keep, cube.core_swap(d_send)], axis=0)
    d_gains = jnp.stack([d_gain_attn, d_gain_ffn]).reshape(2, n, 2 * share)
    d_gains = jnp.transpose(d_gains, (1, 0, 2)).reshape(n, 1, 4 * share).astype(BF16)
    d_gains = jnp.pad(d_gains, ((0, 0), (0, 15), (0, col_half - 4 * share)))
    last = cube.reduce(*picked([split(nn(grouped_t, d_comp_cols, BF16))], d_gains))
    mine = w_compress.shape[0]
    away = jnp.where(core > 0, last[:mine], last[mine : 2 * mine])
    kept = jnp.where(core > 0, last[mine : 2 * mine], last[:mine])
    arrived = cube.core_swap(jnp.concatenate([away, last[2 * mine : 2 * mine + 8]], axis=0))
    grad_compress = by_core(kept, arrived[:mine], 1)
    gain_sum = (last[2 * mine] + arrived[mine])[: 4 * share].reshape(2, 2, share)
    gain_sum = jnp.where(core > 0, gain_sum[:, 1], gain_sum[:, 0])
    return (
        layer_output[None],
        input_grad[None],
        grad_query,
        grad_key,
        grad_value,
        grad_output,
        grad_compress,
        gain_sum[0],
        gain_sum[1],
        grad_inner,
        grad_outer,
        branch_rms,
    )


def solution(mesh):
    in_specs = (
        P("dp", "tensor", None),
        P("dp", "tensor", None),
        P("dp", "tensor", None),
        P("dp"),
        P("dp", None),
        P("dp", "tensor"),
        P("dp", "tensor"),
        P("dp", "tensor"),
        P("tensor", "dp"),
        P(("dp", "tensor"), None),
        P(("dp", "tensor")),
        P(("dp", "tensor")),
        P("dp", "tensor"),
        P("tensor", "dp"),
        P("dp", "tensor", None),
    )
    out_specs = (
        P("dp", "tensor", None),
        P("dp", "tensor", None),
        P("dp", "tensor"),
        P("dp", "tensor"),
        P("dp", "tensor"),
        P("tensor", "dp"),
        P(("dp", "tensor"), None),
        P(("dp", "tensor")),
        P(("dp", "tensor")),
        P("dp", "tensor"),
        P("tensor", "dp"),
        P("dp", None),
    )

    return jax.shard_map(
        per_device, mesh=mesh, in_specs=in_specs, out_specs=out_specs, check_vma=False
    )
```

profile of v0, /device:TPU:0, one launch (start us, length us, event | category | flops | bytes accessed | tf_op | source)
XLA Modules:
  0.0 580.8 jit_solution(16015087432121918791)
XLA Ops:
  11.4 5.1 collective-permute-start.5
  17.2 9.8 %collective-permute-done.5 = bf16[1,64,3200]{2,1,0:T(8,128)(2,1)S(1)} collective-permute-done((bf16[1,64,3200]{2,1,0:T(8,128)(2,1)S(1)}, bf16[1,64,3200]{2,1,0:T(8,128)(2,1)S(1)}, u32[]{:S(2)}, u32[]{:S(2)}) %collective-permute-start.5) | collective-permute-done | bytes 409632 | tf_op jit(solution)/shard_map/ppermute | solution.py:66
  27.0 24.7 %collective-permute-done.4 = bf16[1,64,3200]{2,1,0:T(8,128)(2,1)S(1)} collective-permute-done((bf16[1,64,3200]{2,1,0:T(8,128)(2,1)S(1)}, bf16[1,64,3200]{2,1,0:T(8,128)(2,1)S(1)}, u32[]{:S(2)}, u32[]{:S(2)}) %collective-permute-start.4) | collective-permute-done | bytes 409632 | tf_op jit(solution)/shard_map/ppermute | solution.py:66
  56.7 16.4 %collective-permute-done.6 = bf16[4,64,3200]{2,1,0:T(8,128)(2,1)S(1)} collective-permute-done((bf16[4,64,3200]{2,1,0:T(8,128)(2,1)S(1)}, bf16[4,64,3200]{2,1,0:T(8,128)(2,1)S(1)}, u32[]{:S(2)}, u32[]{:S(2)}) %collective-permute-start.6) | collective-permute-done | bytes 1638432 | tf_op jit(solution)/shard_map/ppermute | solution.py:66
  90.8 14.0 %collective-permute-done.11 = bf16[1,64,2560]{2,1,0:T(8,128)(2,1)} collective-permute-done((bf16[1,64,2560]{2,1,0:T(8,128)(2,1)}, bf16[1,64,2560]{2,1,0:T(8,128)(2,1)}, u32[]{:S(2)}, u32[]{:S(2)}) %collective-permute-start.11) | collective-permute-done | bytes 327712 | tf_op jit(solution)/shard_map/ppermute | solution.py:66
  118.8 7.3 %place.3 = (bf16[16,64,512]{2,1,0:T(8,128)(2,1)}, bf16[16,64,1024]{2,1,0:T(8,128)(2,1)}, bf16[16,64,128]{2,1,0:T(8,128)(2,1)}, bf16[16,192,512]{2,1,0:T(8,128)(2,1)}) custom-call(s32[16]{0:T(128)} %xor_bitcast_fusion.where_ref, bf16[8,64,3200]{2,1,0:T(8,128)(2,1)} %constant_dynamic-update-slice_fusion.12.refs_0_, ...), custom_call_target="tpu_custom_call" | custom-call | tf_op jit(solution)/shard_map/place/pallas_call | solution.py:132
  154.8 14.5 %collective-permute-done.18 = bf16[1,64,2048]{2,1,0:T(8,128)(2,1)S(1)} collective-permute-done((bf16[1,64,2048]{2,1,0:T(8,128)(2,1)S(1)}, bf16[1,64,2048]{2,1,0:T(8,128)(2,1)S(1)}, u32[]{:S(2)}, u32[]{:S(2)}) %collective-permute-start.18) | collective-permute-done | bytes 262176 | tf_op jit(solution)/shard_map/ppermute | solution.py:66
  170.9 5.9 %place.4 = (bf16[16,64,512]{2,1,0:T(8,128)(2,1)}, bf16[16,64,2048]{2,1,0:T(8,128)(2,1)}) custom-call(s32[16]{0:T(128)} %xor_bitcast_fusion.where_ref, bf16[8,64,2560]{2,1,0:T(8,128)(2,1)} %constant_dynamic-update-slice_fusion.17.refs_0_, bf16[8,64,2560]{2,1,0:T(8,128)(2,1)} %collective-permute-done.14.refs_1_), custom_call_target="tpu_custom_call" | custom-call | tf_op jit(solution)/shard_map/place/pallas_call | solution.py:132
  180.0 8.9 %convolution_convert_fusion.3.kv_ref = bf16[2048,1024]{1,0:T(8,128)(2,1)} fusion(bf16[1024,1024]{1,0:T(8,128)(2,1)S(1)} %bitcast.144, bf16[1024,1024]{0,1:T(8,128)(2,1)} %collective-permute-done.9, bf16[1024,1024]{0,1:T(8,128)(2,1)} %multiply_convert_fusion.1), kind=kOutput, calls=%fused_computation.21 | convolution fusion | flops 4305453056 | bytes 10485760 | tf_op jit(solution)/shard_map/dot_general | solution.py:26
  191.2 40.0 %attend.1 = (bf16[1024,512]{1,0:T(8,128)(2,1)}, f32[8,1,512]{2,1,0:T(1,128)}) custom-call(s32[4]{0:T(128)} %pad_add_fusion.info_ref, bf16[1024,512]{1,0:T(8,128)(2,1)} %convolution_convert_fusion.7.q_ref, bf16[2048,1024]{1,0:T(8,128)(2,1)} %convolution_convert_fusion.3.kv_ref), custom_call_target="tpu_custom_call" | custom-call | tf_op jit(solution)/shard_map/attend/pallas_call | solution.py:281
  245.6 18.4 %collective-permute-done.21.refs_1_ = bf16[8,64,2048]{2,1,0:T(8,128)(2,1)} collective-permute-done((bf16[8,64,2048]{2,1,0:T(8,128)(2,1)}, bf16[8,64,2048]{2,1,0:T(8,128)(2,1)}, u32[]{:S(2)}, u32[]{:S(2)}) %collective-permute-start.21) | collective-permute-done | bytes 2097184 | tf_op jit(solution)/shard_map/ppermute | solution.py:66
  264.1 5.0 place.5
  269.1 9.6 %multiply_convert_fusion = (bf16[1024,2048]{1,0:T(8,128)(2,1)S(1)}, f32[1024,2048]{1,0:T(8,128)S(1)}) fusion(bf16[1024,2048]{1,0:T(8,128)(2,1)} %bitcast.139, bf16[512,1024]{0,1:T(8,128)(2,1)} %collective-permute-done.16, bf16[512,1024]{0,1:T(8,128)(2,1)} %multiply_convert_fusion.2), kind=kOutput, calls=%fused_computation.9 | convolution fusion | flops 4318035968 | bytes 18874368 | tf_op jit(solution)/shard_map/dot_general | solution.py:26
  278.8 10.5 %fusion.6 = bf16[1024,2048]{1,0:T(8,128)(2,1)S(1)} fusion(f32[1024,2048]{1,0:T(8,128)S(1)} %get-tuple-element.140, bf16[1024,2048]{1,0:T(8,128)(2,1)S(1)} %bitcast.113, bf16[512,1024]{0,1:T(8,128)(2,1)} %collective-permute-done.23, bf16[512,1024]{0,1:T(8,128)(2,1)S(1)} %bitcast.110), kind=kOutput, calls=%fused_computation.8 | convolution fusion | flops 4341104640 | bytes 18874368 | tf_op jit(solution)/shard_map/dot_general | solution.py:26
  297.1 5.1 multiply_reduce_fusion.4
  304.1 7.5 %convolution_convert_fusion.1 = bf16[1024,2048]{1,0:T(8,128)(2,1)} fusion(bf16[1024,2048]{1,0:T(8,128)(2,1)S(1)} %get-tuple-element.139, bf16[512,1024]{0,1:T(8,128)(2,1)} %collective-permute-done.23, bf16[512,1024]{0,1:T(8,128)(2,1)S(1)} %bitcast.111), kind=kOutput, calls=%fused_computation.19 | convolution fusion | flops 4301258752 | bytes 10485760 | tf_op jit(solution)/shard_map/dot_general | solution.py:26
  311.6 4.9 pick.7
  317.3 9.3 %convolution_convert_fusion.2 = bf16[1024,2048]{1,0:T(8,128)(2,1)} fusion(bf16[1024,2048]{1,0:T(8,128)(2,1)} %copy-done.51, bf16[512,1024]{0,1:T(8,128)(2,1)} %collective-permute-done.16, bf16[512,1024]{0,1:T(8,128)(2,1)} %multiply_convert_fusion.2), kind=kOutput, calls=%fused_computation.20 | convolution fusion | flops 4301258752 | bytes 10485760 | tf_op jit(solution)/shard_map/dot_general | solution.py:26
  334.2 16.5 %attend_back.2 = (bf16[1024,512]{1,0:T(8,128)(2,1)}, bf16[2048,1024]{1,0:T(8,128)(2,1)}) custom-call(s32[4]{0:T(128)} %pad_add_fusion.info_ref, bf16[1024,512]{1,0:T(8,128)(2,1)} %convolution_convert_fusion.7.q_ref, bf16[2048,1024]{1,0:T(8,128)(2,1)} %convolution_convert_fusion.3.kv_ref, bf16[1024,512]{1,0:T(8,128)(2,1)} %get-tuple-element.38.o_ref, ...), custom_call_target="tpu_custom_call" | custom-call | tf_op jit(solution)/shard_map/attend_back/pallas_call | solution.py:360
  350.8 16.9 %attend_back.3 = (bf16[1024,512]{1,0:T(8,128)(2,1)}, bf16[2048,1024]{1,0:T(8,128)(2,1)}) custom-call(s32[4]{0:T(128)} %pad_add_fusion.info_ref, bf16[1024,512]{1,0:T(8,128)(2,1)} %convolution_convert_fusion.7.q_ref, bf16[2048,1024]{1,0:T(8,128)(2,1)} %convolution_convert_fusion.3.kv_ref, ...), custom_call_target="tpu_custom_call", output_to_operand_aliasing={{0}: (6, {}), {1}: (7, {})} | custom-call | tf_op jit(solution)/shard_map/attend_back/pallas_call | solution.py:360
  371.5 8.0 %fusion.19 = bf16[1024,1024]{1,0:T(8,128)(2,1)} fusion(bf16[2048,1024]{1,0:T(8,128)(2,1)S(1)} %copy-done.16, bf16[1024,1024]{0,1:T(8,128)(2,1)} %collective-permute-done.9, bf16[1024,1024]{0,1:T(8,128)(2,1)} %multiply_convert_fusion.1), kind=kOutput, calls=%fused_computation.58 | convolution fusion | flops 4304404480 | bytes 10485760 | tf_op jit(solution)/shard_map/dot_general | solution.py:26
  385.4 7.2 %fusion.90 = f32[2048,1024]{0,1:T(8,128)S(1)} fusion(bf16[2048,1024]{1,0:T(8,128)(2,1)} %get-tuple-element.48, bf16[1024,1024]{1,0:T(8,128)(2,1)} %bitcast.143), kind=kOutput, calls=%fused_computation.219 | convolution fusion | flops 4294967296 | bytes 14680064 | tf_op jit(solution)/shard_map/dot_general | solution.py:26
  406.8 8.8 %collective-permute-done.45 = bf16[4,64,2048]{2,1,0:T(8,128)(2,1)S(1)} collective-permute-done((bf16[4,64,2048]{2,1,0:T(8,128)(2,1)S(1)}, bf16[4,64,2048]{2,1,0:T(8,128)(2,1)S(1)}, u32[]{:S(2)}, u32[]{:S(2)}) %collective-permute-start.45) | collective-permute-done | bytes 1048608 | tf_op jit(solution)/shard_map/ppermute | solution.py:66
  426.1 5.8 %pick.5 = (bf16[8,64,2560]{2,1,0:T(8,128)(2,1)}, bf16[8,64,2560]{2,1,0:T(8,128)(2,1)}) custom-call(s32[16]{0:T(128)} %xor_bitcast_fusion.where_ref, bf16[16,64,512]{2,1,0:T(8,128)(2,1)} %bitcast.124, bf16[16,64,2048]{2,1,0:T(8,128)(2,1)} %bitcast.112), custom_call_target="tpu_custom_call" | custom-call | tf_op jit(solution)/shard_map/pick/pallas_call | solution.py:170
  436.1 7.7 %collective-permute-done.47 = bf16[1,64,2048]{2,1,0:T(8,128)(2,1)} collective-permute-done((bf16[1,64,2048]{2,1,0:T(8,128)(2,1)S(1)}, bf16[1,64,2048]{2,1,0:T(8,128)(2,1)}, u32[]{:S(2)}, u32[]{:S(2)}) %collective-permute-start.47) | collective-permute-done | bytes 262176 | tf_op jit(solution)/shard_map/ppermute | solution.py:66
  455.5 5.6 fusion.84
  464.8 5.7 collective-permute-done.28
  476.0 5.5 convolution_convert_fusion
  486.1 5.4 collective-permute-start.38
  503.7 22.0 %collective-permute-done.38 = bf16[8,208,512]{2,1,0:T(8,128)(2,1)} collective-permute-done((bf16[8,208,512]{2,1,0:T(8,128)(2,1)}, bf16[8,208,512]{2,1,0:T(8,128)(2,1)}, u32[]{:S(2)}, u32[]{:S(2)}) %collective-permute-start.38) | collective-permute-done | bytes 1703968 | tf_op jit(solution)/shard_map/ppermute | solution.py:66
  535.4 5.5 collective-permute-done.39
  550.2 21.9 %collective-permute-done.35 = bf16[1,64,2560]{2,1,0:T(8,128)(2,1)S(1)} collective-permute-done((bf16[1,64,2560]{2,1,0:T(8,128)(2,1)S(1)}, bf16[1,64,2560]{2,1,0:T(8,128)(2,1)S(1)}, u32[]{:S(2)}, u32[]{:S(2)}) %collective-permute-start.35) | collective-permute-done | bytes 327712 | tf_op jit(solution)/shard_map/ppermute | solution.py:66
  (310 shorter events, 218.7 us)
Async XLA Ops:
  16.5 35.1 %collective-permute-start.4 = (bf16[1,64,3200]{2,1,0:T(8,128)(2,1)S(1)}, bf16[1,64,3200]{2,1,0:T(8,128)(2,1)S(1)}, u32[]{:S(2)}, u32[]{:S(2)}) collective-permute-start(bf16[1,64,3200]{2,1,0:T(8,128)(2,1)S(1)} %bitcast.120), channel_id=1, source_target_pairs={{0,16},{1,17},{2,18},{3,19},{4,20},{5,21},{6,22},{7,23},{8,24},{9,... | collective-permute-start | bytes 1228808 | tf_op jit(solution)/shard_map/ppermute | solution.py:66
  16.5 35.1 %collective-permute-start.3 = (bf16[1,64,3200]{2,1,0:T(8,128)(2,1)S(1)}, bf16[1,64,3200]{2,1,0:T(8,128)(2,1)S(1)}, u32[]{:S(2)}, u32[]{:S(2)}) collective-permute-start(bf16[1,64,3200]{2,1,0:T(8,128)(2,1)S(1)} %bitcast.121), channel_id=1, source_target_pairs={{0,8},{1,9},{2,10},{3,11},{4,12},{5,13},{6,14},{7,15},{8,0},{9,1},... | collective-permute-start | bytes 1228808 | tf_op jit(solution)/shard_map/ppermute | solution.py:66
  51.9 21.2 %collective-permute-start.6 = (bf16[4,64,3200]{2,1,0:T(8,128)(2,1)S(1)}, bf16[4,64,3200]{2,1,0:T(8,128)(2,1)S(1)}, u32[]{:S(2)}, u32[]{:S(2)}) collective-permute-start(bf16[4,64,3200]{2,1,0:T(8,128)(2,1)S(1)} %pad_maximum_fusion.11), channel_id=1, source_target_pairs={{0,4},{1,3},{2,6},{3,1},{4,0},{5,7},{6,2},{7,5},{8,12},{9,11},{10,... | collective-permute-start | bytes 4915208 | tf_op jit(solution)/shard_map/ppermute | solution.py:66
  74.4 44.4 %collective-permute-start.7 = (bf16[8,64,3200]{2,1,0:T(8,128)(2,1)}, bf16[8,64,3200]{2,1,0:T(8,128)(2,1)}, u32[]{:S(2)}, u32[]{:S(2)}) collective-permute-start(bf16[8,64,3200]{2,1,0:T(8,128)(2,1)} %constant_dynamic-update-slice_fusion.12.refs_0_), channel_id=1, source_target_pairs={{0,2},{1,5},{2,0},{3,7},{4,6},{5,1},{6,4},{7,3},{8,10},{9,13},{10,... | collective-permute-start | bytes 9830408 | tf_op jit(solution)/shard_map/ppermute | solution.py:66
  79.1 25.7 %collective-permute-start.11 = (bf16[1,64,2560]{2,1,0:T(8,128)(2,1)}, bf16[1,64,2560]{2,1,0:T(8,128)(2,1)}, u32[]{:S(2)}, u32[]{:S(2)}) collective-permute-start(bf16[1,64,2560]{2,1,0:T(8,128)(2,1)} %maximum_bitcast_fusion), channel_id=1, source_target_pairs={{0,16},{1,17},{2,18},{3,19},{4,20},{5,21},{6,22},{7,23},{8,24},{9,... | collective-permute-start | bytes 983048 | tf_op jit(solution)/shard_map/ppermute | solution.py:66
  79.1 25.7 %collective-permute-start.10 = (bf16[1,64,2560]{2,1,0:T(8,128)(2,1)}, bf16[1,64,2560]{2,1,0:T(8,128)(2,1)}, u32[]{:S(2)}, u32[]{:S(2)}) collective-permute-start(bf16[1,64,2560]{2,1,0:T(8,128)(2,1)} %maximum_bitcast_fusion), channel_id=1, source_target_pairs={{0,8},{1,9},{2,10},{3,11},{4,12},{5,13},{6,14},{7,15},{8,0},{9,1},... | collective-permute-start | bytes 983048 | tf_op jit(solution)/shard_map/ppermute | solution.py:66
  82.7 29.2 %collective-permute-start = (bf16[256,3072]{1,0:T(8,128)(2,1)}, bf16[256,3072]{1,0:T(8,128)(2,1)}, u32[]{:S(2)}, u32[]{:S(2)}) collective-permute-start(bf16[256,3072]{1,0:T(8,128)(2,1)} %reshape_squeeze.4), channel_id=1, source_target_pairs={{0,1},{1,0},{2,3},{3,2},{4,5},{5,4},{6,7},{7,6},{8,9},{9,8},{10,11... | collective-permute-start | bytes 4718600 | tf_op jit(solution)/shard_map/ppermute | solution.py:75
  107.2 25.4 %collective-permute-start.13 = (bf16[4,64,2560]{2,1,0:T(8,128)(2,1)}, bf16[4,64,2560]{2,1,0:T(8,128)(2,1)}, u32[]{:S(2)}, u32[]{:S(2)}) collective-permute-start(bf16[4,64,2560]{2,1,0:T(8,128)(2,1)} %pad_maximum_fusion.22), channel_id=1, source_target_pairs={{0,4},{1,3},{2,6},{3,1},{4,0},{5,7},{6,2},{7,5},{8,12},{9,11},{10,... | collective-permute-start | bytes 3932168 | tf_op jit(solution)/shard_map/ppermute | solution.py:66
  135.2 35.8 %collective-permute-start.14 = (bf16[8,64,2560]{2,1,0:T(8,128)(2,1)}, bf16[8,64,2560]{2,1,0:T(8,128)(2,1)}, u32[]{:S(2)}, u32[]{:S(2)}) collective-permute-start(bf16[8,64,2560]{2,1,0:T(8,128)(2,1)} %constant_dynamic-update-slice_fusion.17.refs_0_), channel_id=1, source_target_pairs={{0,2},{1,5},{2,0},{3,7},{4,6},{5,1},{6,4},{7,3},{8,10},{9,13},{10,... | collective-permute-start | bytes 7864328 | tf_op jit(solution)/shard_map/ppermute | solution.py:66
  141.3 36.9 %collective-permute-start.9 = (bf16[1024,1024]{0,1:T(8,128)(2,1)}, bf16[1024,1024]{0,1:T(8,128)(2,1)}, u32[]{:S(2)}, u32[]{:S(2)}) collective-permute-start(bf16[1024,1024]{0,1:T(8,128)(2,1)} %multiply_convert_fusion.1), channel_id=1, source_target_pairs={{0,1},{1,0},{2,3},{3,2},{4,5},{5,4},{6,7},{7,6},{8,9},{9,8},{10,11... | collective-permute-start | bytes 6291464 | tf_op jit(solution)/shard_map/ppermute | solution.py:75
  147.5 21.8 %collective-permute-start.18 = (bf16[1,64,2048]{2,1,0:T(8,128)(2,1)S(1)}, bf16[1,64,2048]{2,1,0:T(8,128)(2,1)S(1)}, u32[]{:S(2)}, u32[]{:S(2)}) collective-permute-start(bf16[1,64,2048]{2,1,0:T(8,128)(2,1)S(1)} %bitcast.126), channel_id=1, source_target_pairs={{0,16},{1,17},{2,18},{3,19},{4,20},{5,21},{6,22},{7,23},{8,24},{9,... | collective-permute-start | bytes 786440 | tf_op jit(solution)/shard_map/ppermute | solution.py:66
  147.5 21.8 %collective-permute-start.17 = (bf16[1,64,2048]{2,1,0:T(8,128)(2,1)S(1)}, bf16[1,64,2048]{2,1,0:T(8,128)(2,1)S(1)}, u32[]{:S(2)}, u32[]{:S(2)}) collective-permute-start(bf16[1,64,2048]{2,1,0:T(8,128)(2,1)S(1)} %bitcast.127), channel_id=1, source_target_pairs={{0,8},{1,9},{2,10},{3,11},{4,12},{5,13},{6,14},{7,15},{8,0},{9,1},... | collective-permute-start | bytes 786440 | tf_op jit(solution)/shard_map/ppermute | solution.py:66
  169.4 67.2 %collective-permute-start.20 = (bf16[4,64,2048]{2,1,0:T(8,128)(2,1)S(1)}, bf16[4,64,2048]{2,1,0:T(8,128)(2,1)S(1)}, u32[]{:S(2)}, u32[]{:S(2)}) collective-permute-start(bf16[4,64,2048]{2,1,0:T(8,128)(2,1)S(1)} %pad_maximum_fusion.23), channel_id=1, source_target_pairs={{0,4},{1,3},{2,6},{3,1},{4,0},{5,7},{6,2},{7,5},{8,12},{9,11},{10,... | collective-permute-start | bytes 3145736 | tf_op jit(solution)/shard_map/ppermute | solution.py:66
  237.7 26.4 %collective-permute-start.21 = (bf16[8,64,2048]{2,1,0:T(8,128)(2,1)}, bf16[8,64,2048]{2,1,0:T(8,128)(2,1)}, u32[]{:S(2)}, u32[]{:S(2)}) collective-permute-start(bf16[8,64,2048]{2,1,0:T(8,128)(2,1)} %constant_dynamic-update-slice_fusion.22.refs_0_), channel_id=1, source_target_pairs={{0,2},{1,5},{2,0},{3,7},{4,6},{5,1},{6,4},{7,3},{8,10},{9,13},{10,... | collective-permute-start | bytes 6291464 | tf_op jit(solution)/shard_map/ppermute | solution.py:66
  243.5 25.6 %collective-permute-start.16 = (bf16[512,1024]{0,1:T(8,128)(2,1)}, bf16[512,1024]{0,1:T(8,128)(2,1)}, u32[]{:S(2)}, u32[]{:S(2)}) collective-permute-start(bf16[512,1024]{0,1:T(8,128)(2,1)} %multiply_convert_fusion.2), channel_id=1, source_target_pairs={{0,1},{1,0},{2,3},{3,2},{4,5},{5,4},{6,7},{7,6},{8,9},{9,8},{10,11... | collective-permute-start | bytes 3145736 | tf_op jit(solution)/shard_map/ppermute | solution.py:75
  245.1 33.7 %collective-permute-start.23 = (bf16[512,1024]{0,1:T(8,128)(2,1)S(1)}, bf16[512,1024]{0,1:T(8,128)(2,1)}, u32[]{:S(2)}, u32[]{:S(2)}) collective-permute-start(bf16[512,1024]{0,1:T(8,128)(2,1)S(1)} %bitcast.109), channel_id=1, source_target_pairs={{0,1},{1,0},{2,3},{3,2},{4,5},{5,4},{6,7},{7,6},{8,9},{9,8},{10,11... | collective-permute-start | bytes 3145736 | tf_op jit(solution)/shard_map/ppermute | solution.py:75
  303.8 26.3 %collective-permute-start.25 = (bf16[512,1024]{0,1:T(8,128)(2,1)}, bf16[512,1024]{0,1:T(8,128)(2,1)}, u32[]{:S(2)}, u32[]{:S(2)}) collective-permute-start(bf16[512,1024]{0,1:T(8,128)(2,1)} %fusion.83), channel_id=1, source_target_pairs={{0,1},{1,0},{2,3},{3,2},{4,5},{5,4},{6,7},{7,6},{8,9},{9,8},{10,11... | collective-permute-start | bytes 3145736 | tf_op jit(solution)/shard_map/ppermute | solution.py:75
  316.5 76.3 %collective-permute-start.44 = (bf16[8,64,2048]{2,1,0:T(8,128)(2,1)}, bf16[8,64,2048]{2,1,0:T(8,128)(2,1)S(1)}, u32[]{:S(2)}, u32[]{:S(2)}) collective-permute-start(bf16[8,64,2048]{2,1,0:T(8,128)(2,1)} %get-tuple-element.55), channel_id=1, source_target_pairs={{0,2},{1,5},{2,0},{3,7},{4,6},{5,1},{6,4},{7,3},{8,10},{9,13},{10,... | collective-permute-start | bytes 6291464 | tf_op jit(solution)/shard_map/ppermute | solution.py:66
  328.8 75.4 %collective-permute-start.49 = (f32[3]{0:T(128)S(1)}, f32[3]{0:T(128)S(1)}, u32[]{:S(2)}, u32[]{:S(2)}) collective-permute-start(f32[3]{0:T(128)S(1)} %pad_maximum_fusion.31), channel_id=1, source_target_pairs={{0,1},{1,0},{2,3},{3,2},{4,5},{5,4},{6,7},{7,6},{8,9},{9,8},{10,11... | collective-permute-start | bytes 44 | tf_op jit(solution)/shard_map/ppermute | solution.py:75
  384.1 61.9 %collective-permute-start.27 = (bf16[8,64,1536]{2,1,0:T(8,128)(2,1)}, bf16[8,64,1536]{2,1,0:T(8,128)(2,1)}, u32[]{:S(2)}, u32[]{:S(2)}) collective-permute-start(bf16[8,64,1536]{2,1,0:T(8,128)(2,1)} %get-tuple-element.47), channel_id=1, source_target_pairs={{0,2},{1,5},{2,0},{3,7},{4,6},{5,1},{6,4},{7,3},{8,10},{9,13},{10,... | collective-permute-start | bytes 4718600 | tf_op jit(solution)/shard_map/ppermute | solution.py:66
  404.1 47.5 %collective-permute-start.26 = (bf16[1024,1024]{0,1:T(8,128)(2,1)}, bf16[1024,1024]{0,1:T(8,128)(2,1)}, u32[]{:S(2)}, u32[]{:S(2)}) collective-permute-start(bf16[1024,1024]{0,1:T(8,128)(2,1)} %pad_maximum_fusion.8), channel_id=1, source_target_pairs={{0,1},{1,0},{2,3},{3,2},{4,5},{5,4},{6,7},{7,6},{8,9},{9,8},{10,11... | collective-permute-start | bytes 6291464 | tf_op jit(solution)/shard_map/ppermute | solution.py:75
  422.3 21.4 %collective-permute-start.47 = (bf16[1,64,2048]{2,1,0:T(8,128)(2,1)S(1)}, bf16[1,64,2048]{2,1,0:T(8,128)(2,1)}, u32[]{:S(2)}, u32[]{:S(2)}) collective-permute-start(bf16[1,64,2048]{2,1,0:T(8,128)(2,1)S(1)} %get-tuple-element.109), channel_id=1, source_target_pairs={{0,16},{1,17},{2,18},{3,19},{4,20},{5,21},{6,22},{7,23},{8,24},{9,... | collective-permute-start | bytes 786440 | tf_op jit(solution)/shard_map/ppermute | solution.py:66
  431.9 59.6 %collective-permute-start.32 = (bf16[8,64,2560]{2,1,0:T(8,128)(2,1)}, bf16[8,64,2560]{2,1,0:T(8,128)(2,1)}, u32[]{:S(2)}, u32[]{:S(2)}) collective-permute-start(bf16[8,64,2560]{2,1,0:T(8,128)(2,1)} %get-tuple-element.51), channel_id=1, source_target_pairs={{0,2},{1,5},{2,0},{3,7},{4,6},{5,1},{6,4},{7,3},{8,10},{9,13},{10,... | collective-permute-start | bytes 7864328 | tf_op jit(solution)/shard_map/ppermute | solution.py:66
  472.5 30.0 %collective-permute-start.29 = (bf16[1,64,1536]{2,1,0:T(8,128)(2,1)}, bf16[1,64,1536]{2,1,0:T(8,128)(2,1)S(1)}, u32[]{:S(2)}, u32[]{:S(2)}) collective-permute-start(bf16[1,64,1536]{2,1,0:T(8,128)(2,1)} %get-tuple-element.115), channel_id=1, source_target_pairs={{0,8},{1,9},{2,10},{3,11},{4,12},{5,13},{6,14},{7,15},{8,0},{9,1},... | collective-permute-start | bytes 589832 | tf_op jit(solution)/shard_map/ppermute | solution.py:66
  472.5 30.0 %collective-permute-start.31 = (bf16[1,64,1536]{2,1,0:T(8,128)(2,1)S(1)}, bf16[1,64,1536]{2,1,0:T(8,128)(2,1)S(1)}, u32[]{:S(2)}, u32[]{:S(2)}) collective-permute-start(bf16[1,64,1536]{2,1,0:T(8,128)(2,1)S(1)} %get-tuple-element.116), channel_id=1, source_target_pairs={{0,24},{1,25},{2,26},{3,27},{4,28},{5,29},{6,30},{7,31},{8,16},{9,... | collective-permute-start | bytes 589832 | tf_op jit(solution)/shard_map/ppermute | solution.py:66
  475.0 27.4 %collective-permute-start.30 = (bf16[1,64,1536]{2,1,0:T(8,128)(2,1)S(1)}, bf16[1,64,1536]{2,1,0:T(8,128)(2,1)}, u32[]{:S(2)}, u32[]{:S(2)}) collective-permute-start(bf16[1,64,1536]{2,1,0:T(8,128)(2,1)S(1)} %get-tuple-element.117), channel_id=1, source_target_pairs={{0,16},{1,17},{2,18},{3,19},{4,20},{5,21},{6,22},{7,23},{8,24},{9,... | collective-permute-start | bytes 589832 | tf_op jit(solution)/shard_map/ppermute | solution.py:66
  486.1 39.5 %collective-permute-start.38 = (bf16[8,208,512]{2,1,0:T(8,128)(2,1)}, bf16[8,208,512]{2,1,0:T(8,128)(2,1)}, u32[]{:S(2)}, u32[]{:S(2)}) collective-permute-start(bf16[8,208,512]{2,1,0:T(8,128)(2,1)} %get-tuple-element.53), channel_id=1, source_target_pairs={{0,2},{1,5},{2,0},{3,7},{4,6},{5,1},{6,4},{7,3},{8,10},{9,13},{10,... | collective-permute-start | bytes 5111816 | tf_op jit(solution)/shard_map/ppermute | solution.py:66
  496.0 33.7 %collective-permute-start.33 = (bf16[4,64,2560]{2,1,0:T(8,128)(2,1)}, bf16[4,64,2560]{2,1,0:T(8,128)(2,1)}, u32[]{:S(2)}, u32[]{:S(2)}) collective-permute-start(bf16[4,64,2560]{2,1,0:T(8,128)(2,1)} %get-tuple-element.97), channel_id=1, source_target_pairs={{0,4},{1,3},{2,6},{3,1},{4,0},{5,7},{6,2},{7,5},{8,12},{9,11},{10,... | collective-permute-start | bytes 3932168 | tf_op jit(solution)/shard_map/ppermute | solution.py:66
  534.6 37.5 %collective-permute-start.35 = (bf16[1,64,2560]{2,1,0:T(8,128)(2,1)S(1)}, bf16[1,64,2560]{2,1,0:T(8,128)(2,1)S(1)}, u32[]{:S(2)}, u32[]{:S(2)}) collective-permute-start(bf16[1,64,2560]{2,1,0:T(8,128)(2,1)S(1)} %get-tuple-element.104), channel_id=1, source_target_pairs={{0,16},{1,17},{2,18},{3,19},{4,20},{5,21},{6,22},{7,23},{8,24},{9,... | collective-permute-start | bytes 983048 | tf_op jit(solution)/shard_map/ppermute | solution.py:66
  541.1 33.0 %collective-permute-start.40 = (bf16[1,208,512]{2,1,0:T(8,128)(2,1)S(1)}, bf16[1,208,512]{2,1,0:T(8,128)(2,1)S(1)}, u32[]{:S(2)}, u32[]{:S(2)}) collective-permute-start(bf16[1,208,512]{2,1,0:T(8,128)(2,1)S(1)} %get-tuple-element.112), channel_id=1, source_target_pairs={{0,8},{1,9},{2,10},{3,11},{4,12},{5,13},{6,14},{7,15},{8,0},{9,1},... | collective-permute-start | bytes 638984 | tf_op jit(solution)/shard_map/ppermute | solution.py:66
  542.1 32.0 %collective-permute-start.42 = (bf16[1,208,512]{2,1,0:T(8,128)(2,1)S(1)}, bf16[1,208,512]{2,1,0:T(8,128)(2,1)S(1)}, u32[]{:S(2)}, u32[]{:S(2)}) collective-permute-start(bf16[1,208,512]{2,1,0:T(8,128)(2,1)S(1)} %get-tuple-element.113), channel_id=1, source_target_pairs={{0,24},{1,25},{2,26},{3,27},{4,28},{5,29},{6,30},{7,31},{8,16},{9,... | collective-permute-start | bytes 638984 | tf_op jit(solution)/shard_map/ppermute | solution.py:66
  549.7 27.5 %collective-permute-start.41 = (bf16[1,208,512]{2,1,0:T(8,128)(2,1)S(1)}, bf16[1,208,512]{2,1,0:T(8,128)(2,1)S(1)}, u32[]{:S(2)}, u32[]{:S(2)}) collective-permute-start(bf16[1,208,512]{2,1,0:T(8,128)(2,1)S(1)} %get-tuple-element.114), channel_id=1, source_target_pairs={{0,16},{1,17},{2,18},{3,19},{4,20},{5,21},{6,22},{7,23},{8,24},{9,... | collective-permute-start | bytes 638984 | tf_op jit(solution)/shard_map/ppermute | solution.py:66
  (70 other events, 766.7 us)
where the time goes:
time: 591 us; the launch traced here: 581 us
  waiting for transfers between devices  188 us (32%)
  Pallas kernels  112 us (19%)
  matrix products  105 us (18%)
  other arithmetic  62.3 us (11%)
  starting transfers between devices  62 us (10%)
  local copies, waits for them, and re-layouts  49.2 us (8%)
    ppermute x35, waiting for transfers between devices, send(): return lax.ppermute(value, AXES, pairs)  187 us
    dot_general x20, matrix products, matmul(): lax.dot_general(a, b, (dims, ((), ())), preferred_element_type=F32)  105 us
    ppermute x35, starting transfers between devices, send(): return lax.ppermute(value, AXES, pairs)  54.7 us
    pallas_call x1, Pallas kernels, attend(): pl.pallas_call(body, out_shape=(jax.ShapeDtypeStruct(query_rows.shape, BF...  40 us
    pallas_call x2, Pallas kernels, attend_back(): pl.pallas_call(body, out_shape=(jax.ShapeDtypeStruct(query_rows.shape, BF...  33.4 us
    unnamed x132, local copies, waits for them, and re-layouts  31.6 us
    pallas_call x4, Pallas kernels, pick(): pl.pallas_call(body, out_shape=[jax.ShapeDtypeStruct((half, total, width)...  20 us
    pallas_call x3, Pallas kernels, place(): pl.pallas_call(body, out_shape=[jax.ShapeDtypeStruct((count, r, w), parts...  18.2 us
  transfers between devices with their start and end apart: 50, of which 18 were waited for; matrix products, arithmetic and copies ran while one was open for 32% of the time, Pallas kernels for 19%

commit v1 on v0

--- a/solution.py
+++ b/solution.py
@@ -82,10 +82,10 @@
             return part[run].astype(F32) + other[run].astype(F32)
 
         far = slice(half, None)
-        near = added(low, arrived, slice(0, half))
+        near = added(low, arrived, slice(0, half)).astype(BF16)
         far_sum = added(low, arrived, far).astype(BF16)
         arrived = self.low_swap(far_sum, 0)
-        total = near[0] + arrived[0].astype(F32)
+        total = near[0].astype(F32) + arrived[0].astype(F32)
         sent = [
             self.far_send(added(near, arrived, slice(m, m + 1)).astype(BF16), m)
             for m in range(1, self.far)
@@ -229,8 +229,7 @@
     for half in (0, 1):
         chunks.append((start("mem", half), mem_part, tail(half * mem_part, MEM, mem_len), None))
     crosses = (span < tok_part) & (span + PIC > tok_part)
-    chunks.append((start("tok", 0), tok_part, None, q_half == 1))
-    chunks.append((start("tok", 0), tok_part, causal(0), q_half == 0))
+    chunks.append((start("tok", 0), tok_part, causal(0), None))
     chunks.append((start("tok", 1), tok_part, causal(1), (q_half == 1) | crosses))
     return chunks
 
@@ -240,40 +239,60 @@
     q_part = query_rows.shape[0] // 2
     factor = DH ** (-0.5) * LOG2E
 
-    def body(info_ref, q_ref, kv_ref, o_ref, lse_ref, vt_ref, m_ref, l_ref, acc_ref):
+    def body(info_ref, q_ref, kv_ref, o_ref, lse_ref, vt_ref, s_ref, m_ref, l_ref, acc_ref):
         q_half = pl.program_id(1)
 
         @pl.when(q_half == 0)
         def _():
             vt_ref[...] = kv_ref[:, DH:].T
 
-        m_ref[...] = jnp.full_like(m_ref, very_negative)
-        l_ref[...] = jnp.zeros_like(l_ref)
-        acc_ref[...] = jnp.zeros_like(acc_ref)
         q = q_ref[...]
-        for first, count, masker, needed in attention_chunks(info_ref, q_half, shapes):
-
-            def step(first=first, count=count, masker=masker):
-                s = nt(kv_ref[pl.ds(first, count), :DH], q)
-                if masker is not None:
-                    s = jnp.where(masker(s.shape), s, very_negative)
-                m_old = m_ref[...]
-                m_new = jnp.maximum(m_old, jnp.max(s, axis=0, keepdims=True))
-                shrink = jnp.exp2((m_old - m_new) * factor)
-                p = jnp.exp2((s - m_new) * factor)
-                l_ref[...] = l_ref[...] * shrink + jnp.sum(p, axis=0, keepdims=True)
-                acc_ref[...] = acc_ref[...] * shrink + nn(
-                    vt_ref[:, pl.ds(first, count)], p.astype(BF16)
-                )
-                m_ref[...] = m_new
-
-            if needed is None:
-                step()
-            else:
-                pl.when(needed)(step)
-        total = l_ref[...]
+        chunks = attention_chunks(info_ref, q_half, shapes)
+        always = [c for c in chunks if c[3] is None]
+        (first1, count1, masker1, needed1) = next(c for c in chunks if c[3] is not None)
+        spots = [sum(c[1] for c in always[:i]) for i in range(len(always) + 1)]
+
+        def fold(values):
+            return values.reshape(-1, 8, values.shape[1])
+
+        def scores(first, count, masker, spot):
+            s = nt(kv_ref[pl.ds(first, count), :DH], q)
+            s = jnp.where(masker(s.shape), s, very_negative)
+            s_ref[spot : spot + count, :] = s
+            return jnp.max(fold(s), axis=0)
+
+        def weigh(first, count, spot, top):
+            p = jnp.exp2((s_ref[spot : spot + count, :] - top) * factor)
+            return jnp.sum(fold(p), axis=0), nn(vt_ref[:, pl.ds(first, count)], p.astype(BF16))
+
+        peak = None
+        for (first, count, masker, _), spot in zip(always, spots):
+            here = scores(first, count, masker, spot)
+            peak = here if peak is None else jnp.maximum(peak, here)
+        m_ref[...] = peak
+
+        @pl.when(needed1)
+        def _():
+            m_ref[...] = jnp.maximum(m_ref[...], scores(first1, count1, masker1, spots[-1]))
+
+        top = jnp.max(m_ref[...], axis=0, keepdims=True)
+        total, acc = None, None
+        for (first, count, _, _), spot in zip(always, spots):
+            part, product = weigh(first, count, spot, top)
+            total = part if total is None else total + part
+            acc = product if acc is None else acc + product
+        l_ref[...] = total
+        acc_ref[...] = acc
+
+        @pl.when(needed1)
+        def _():
+            part, product = weigh(first1, count1, spots[-1], top)
+            l_ref[...] += part
+            acc_ref[...] += product
+
+        total = jnp.sum(l_ref[...], axis=0, keepdims=True)
         o_ref[...] = (acc_ref[...] / total).T.astype(BF16)
-        lse_ref[...] = (m_ref[...] * factor + jnp.log2(total))[None]
+        lse_ref[...] = (top * factor + jnp.log2(total))[None]
 
     def q_map(h, a, info_ref):
         return (jnp.bitwise_xor(a, info_ref[0]), h)
@@ -297,8 +316,9 @@
             ],
             scratch_shapes=[
                 pltpu.VMEM((DH, rows), BF16),
-                pltpu.VMEM((1, q_part), F32),
-                pltpu.VMEM((1, q_part), F32),
+                pltpu.VMEM((rows, q_part), F32),
+                pltpu.VMEM((8, q_part), F32),
+                pltpu.VMEM((8, q_part), F32),
                 pltpu.VMEM((DH, q_part), F32),
             ],
         ),
@@ -418,10 +438,10 @@
     def gathered(shard, pieces, outs):
         held = [shard[None]] + [cube.far_send(shard[None], m) for m in range(1, cube.far)]
         held = jnp.concatenate(held, axis=0)
-        arrived = cube.low_swap(held, 0)
-        held = jnp.concatenate([held, arrived], axis=0)
-        arrived = cube.low_swap(held, 1)
-        return place([held, arrived], cube.own, pieces, outs)
+        near = cube.low_swap(held, 0)
+        own_far = cube.low_swap(held, 1)
+        far = cube.low_swap(near, 1)
+        return place([held, near, own_far, far], cube.own, pieces, outs)
 
     def picked(blocks, below=None):
         return pick(blocks, cube.own, below)

time: 591 us -> 579 us (0.980)
  Pallas kernels: 112 us -> 91.6 us
  starting transfers between devices: 62 us -> 82.2 us
  local copies, waits for them, and re-layouts: 49.2 us -> 31.7 us
    pallas_call x1, Pallas kernels: 40 us -> 19.9 us  [attend(): pl.pallas_call(body, out_shape=(jax.ShapeDtypeStruct(query_rows.shape, BF...]
    ppermute x35 -> x38, starting transfers between devices: 54.7 us -> 72.5 us  [send(): return lax.ppermute(value, AXES, pairs)]
    unnamed x132 -> x119, local copies, waits for them, and re-layouts: 31.6 us -> 19.1 us
    ppermute x35 -> x38, waiting for transfers between devices: 187 us -> 191 us  [send(): return lax.ppermute(value, AXES, pairs)]
  transfers between devices with their start and end apart: 50 -> 53, of which waited for: 18 -> 21; matrix products, arithmetic and copies ran while one was open for 32% -> 30% of each run, Pallas kernels for 19% -> 16%
where the time goes in v1:
time: 579 us; the launch traced here: 569 us
  waiting for transfers between devices  193 us (33%)
  matrix products  103 us (18%)
  Pallas kernels  91.6 us (16%)
  starting transfers between devices  82.2 us (14%)
  other arithmetic  64.8 us (11%)
  local copies, waits for them, and re-layouts  31.7 us (5%)
    ppermute x38, waiting for transfers between devices, send(): return lax.ppermute(value, AXES, pairs)  191 us
    dot_general x20, matrix products, matmul(): lax.dot_general(a, b, (dims, ((), ())), preferred_element_type=F32)  103 us
    ppermute x38, starting transfers between devices, send(): return lax.ppermute(value, AXES, pairs)  72.5 us
    pallas_call x2, Pallas kernels, attend_back(): pl.pallas_call(body, out_shape=(jax.ShapeDtypeStruct(query_rows.shape, BF...  33.4 us
    pallas_call x4, Pallas kernels, pick(): pl.pallas_call(body, out_shape=[jax.ShapeDtypeStruct((half, total, width)...  20.2 us
    pallas_call x1, Pallas kernels, attend(): pl.pallas_call(body, out_shape=(jax.ShapeDtypeStruct(query_rows.shape, BF...  19.9 us
    unnamed x119, local copies, waits for them, and re-layouts  19.1 us
    pallas_call x3, Pallas kernels, place(): pl.pallas_call(body, out_shape=[jax.ShapeDtypeStruct((count, r, w), parts...  18.1 us
  transfers between devices with their start and end apart: 53, of which 21 were waited for; matrix products, arithmetic and copies ran while one was open for 30% of the time, Pallas kernels for 16%

profile of v1, /device:TPU:0, one launch (start us, length us, event | category | flops | bytes accessed | tf_op | source)
XLA Modules:
  0.0 568.8 jit_solution(15538007247076952690)
XLA Ops:
  11.5 5.1 collective-permute-start.5
  17.3 9.8 %collective-permute-done.5 = bf16[1,64,3200]{2,1,0:T(8,128)(2,1)S(1)} collective-permute-done((bf16[1,64,3200]{2,1,0:T(8,128)(2,1)S(1)}, bf16[1,64,3200]{2,1,0:T(8,128)(2,1)S(1)}, u32[]{:S(2)}, u32[]{:S(2)}) %collective-permute-start.5) | collective-permute-done | bytes 409632 | tf_op jit(solution)/shard_map/ppermute | solution.py:66
  27.1 24.7 %collective-permute-done.4 = bf16[1,64,3200]{2,1,0:T(8,128)(2,1)S(1)} collective-permute-done((bf16[1,64,3200]{2,1,0:T(8,128)(2,1)S(1)}, bf16[1,64,3200]{2,1,0:T(8,128)(2,1)S(1)}, u32[]{:S(2)}, u32[]{:S(2)}) %collective-permute-start.4) | collective-permute-done | bytes 409632 | tf_op jit(solution)/shard_map/ppermute | solution.py:66
  57.9 31.7 %collective-permute-done.6.refs_1_ = bf16[4,64,3200]{2,1,0:T(8,128)(2,1)} collective-permute-done((bf16[4,64,3200]{2,1,0:T(8,128)(2,1)}, bf16[4,64,3200]{2,1,0:T(8,128)(2,1)}, u32[]{:S(2)}, u32[]{:S(2)}) %collective-permute-start.6) | collective-permute-done | bytes 1638432 | tf_op jit(solution)/shard_map/ppermute | solution.py:66
  111.0 7.2 %place.3 = (bf16[16,64,512]{2,1,0:T(8,128)(2,1)}, bf16[16,64,1024]{2,1,0:T(8,128)(2,1)}, bf16[16,64,128]{2,1,0:T(8,128)(2,1)}, bf16[16,192,512]{2,1,0:T(8,128)(2,1)}) custom-call(s32[16]{0:T(128)} %xor_bitcast_fusion.where_ref, bf16[4,64,3200]{2,1,0:T(8,128)(2,1)} %pad_maximum_fusion.11.refs_0_, bf16[4,64,3200]{2,1,0:T(8,128)(2,1)} %collective-permute-done.6.refs_1_, ...), custom_call_target="tpu_custom_call" | custom-call | tf_op jit(solution)/shard_map/place/pallas_call | solution.py:132
  135.4 17.1 %collective-permute-done.14.refs_1_ = bf16[4,64,2560]{2,1,0:T(8,128)(2,1)} collective-permute-done((bf16[4,64,2560]{2,1,0:T(8,128)(2,1)}, bf16[4,64,2560]{2,1,0:T(8,128)(2,1)}, u32[]{:S(2)}, u32[]{:S(2)}) %collective-permute-start.14) | collective-permute-done | bytes 1310752 | tf_op jit(solution)/shard_map/ppermute | solution.py:66
  157.4 8.6 %collective-permute-done.21 = bf16[1,64,2048]{2,1,0:T(8,128)(2,1)S(1)} collective-permute-done((bf16[1,64,2048]{2,1,0:T(8,128)(2,1)S(1)}, bf16[1,64,2048]{2,1,0:T(8,128)(2,1)S(1)}, u32[]{:S(2)}, u32[]{:S(2)}) %collective-permute-start.21) | collective-permute-done | bytes 262176 | tf_op jit(solution)/shard_map/ppermute | solution.py:66
  166.0 8.9 %collective-permute-start.19 = (bf16[1,64,2048]{2,1,0:T(8,128)(2,1)S(1)}, bf16[1,64,2048]{2,1,0:T(8,128)(2,1)S(1)}, u32[]{:S(2)}, u32[]{:S(2)}) collective-permute-start(bf16[1,64,2048]{2,1,0:T(8,128)(2,1)S(1)} %bitcast.125), channel_id=1, source_target_pairs={{0,8},{1,9},{2,10},{3,11},{4,12},{5,13},{6,14},{7,15},{8,0},{9,1},... | collective-permute-start | bytes 786440 | tf_op jit(solution)/shard_map/ppermute | solution.py:66
  183.5 5.8 %place.4 = (bf16[16,64,512]{2,1,0:T(8,128)(2,1)}, bf16[16,64,2048]{2,1,0:T(8,128)(2,1)}) custom-call(s32[16]{0:T(128)} %xor_bitcast_fusion.where_ref, bf16[4,64,2560]{2,1,0:T(8,128)(2,1)} %pad_maximum_fusion.22.refs_0_, bf16[4,64,2560]{2,1,0:T(8,128)(2,1)} %collective-permute-done.14.refs_1_, bf16[4,64,2560]{2,1,0:T(8,128)(2,1)} %copy-done.24, ...), custom_call_target="tpu_custom_call" | custom-call | tf_op jit(solution)/shard_map/place/pallas_call | solution.py:132
  194.8 8.5 %convolution_convert_fusion.3.kv_ref = bf16[2048,1024]{1,0:T(8,128)(2,1)} fusion(bf16[1024,1024]{1,0:T(8,128)(2,1)S(1)} %bitcast.139, bf16[1024,1024]{0,1:T(8,128)(2,1)} %collective-permute-done.10, bf16[1024,1024]{0,1:T(8,128)(2,1)} %multiply_convert_fusion.1), kind=kOutput, calls=%fused_computation.21 | convolution fusion | flops 4305453056 | bytes 10485760 | tf_op jit(solution)/shard_map/dot_general | solution.py:26
  203.3 19.9 %attend.1 = (bf16[1024,512]{1,0:T(8,128)(2,1)}, f32[8,1,512]{2,1,0:T(1,128)}) custom-call(s32[4]{0:T(128)} %pad_add_fusion.info_ref, bf16[1024,512]{1,0:T(8,128)(2,1)} %convolution_convert_fusion.7.q_ref, bf16[2048,1024]{1,0:T(8,128)(2,1)} %convolution_convert_fusion.3.kv_ref), custom_call_target="tpu_custom_call" | custom-call | tf_op jit(solution)/shard_map/attend/pallas_call | solution.py:300
  239.3 5.7 collective-permute-done.23.refs_2_
  245.0 11.2 %collective-permute-done.24.refs_3_ = bf16[4,64,2048]{2,1,0:T(8,128)(2,1)} collective-permute-done((bf16[4,64,2048]{2,1,0:T(8,128)(2,1)}, bf16[4,64,2048]{2,1,0:T(8,128)(2,1)}, u32[]{:S(2)}, u32[]{:S(2)}) %collective-permute-start.24) | collective-permute-done | bytes 1048608 | tf_op jit(solution)/shard_map/ppermute | solution.py:66
  261.3 9.6 %multiply_convert_fusion = (bf16[1024,2048]{1,0:T(8,128)(2,1)S(1)}, f32[1024,2048]{1,0:T(8,128)S(1)}) fusion(bf16[1024,2048]{1,0:T(8,128)(2,1)} %bitcast.134, bf16[512,1024]{0,1:T(8,128)(2,1)} %collective-permute-done.18, bf16[512,1024]{0,1:T(8,128)(2,1)} %multiply_convert_fusion.2), kind=kOutput, calls=%fused_computation.9 | convolution fusion | flops 4318035968 | bytes 18874368 | tf_op jit(solution)/shard_map/dot_general | solution.py:26
  271.0 10.3 %fusion.6 = bf16[1024,2048]{1,0:T(8,128)(2,1)S(1)} fusion(f32[1024,2048]{1,0:T(8,128)S(1)} %get-tuple-element.140, bf16[1024,2048]{1,0:T(8,128)(2,1)S(1)} %bitcast.109, bf16[512,1024]{0,1:T(8,128)(2,1)} %collective-permute-done.26, bf16[512,1024]{0,1:T(8,128)(2,1)S(1)} %bitcast.106), kind=kOutput, calls=%fused_computation.8 | convolution fusion | flops 4341104640 | bytes 18874368 | tf_op jit(solution)/shard_map/dot_general | solution.py:26
  289.0 5.1 multiply_reduce_fusion.4
  296.0 7.6 %convolution_convert_fusion.1 = bf16[1024,2048]{1,0:T(8,128)(2,1)} fusion(bf16[1024,2048]{1,0:T(8,128)(2,1)S(1)} %get-tuple-element.139, bf16[512,1024]{0,1:T(8,128)(2,1)} %collective-permute-done.26, bf16[512,1024]{0,1:T(8,128)(2,1)S(1)} %bitcast.107), kind=kOutput, calls=%fused_computation.19 | convolution fusion | flops 4301258752 | bytes 10485760 | tf_op jit(solution)/shard_map/dot_general | solution.py:26
  308.9 9.4 %convolution_convert_fusion.2 = bf16[1024,2048]{1,0:T(8,128)(2,1)} fusion(bf16[1024,2048]{1,0:T(8,128)(2,1)} %copy-done.50, bf16[512,1024]{0,1:T(8,128)(2,1)} %collective-permute-done.18, bf16[512,1024]{0,1:T(8,128)(2,1)} %multiply_convert_fusion.2), kind=kOutput, calls=%fused_computation.20 | convolution fusion | flops 4301258752 | bytes 10485760 | tf_op jit(solution)/shard_map/dot_general | solution.py:26
  322.1 16.5 %attend_back.2 = (bf16[1024,512]{1,0:T(8,128)(2,1)}, bf16[2048,1024]{1,0:T(8,128)(2,1)}) custom-call(s32[4]{0:T(128)} %pad_add_fusion.info_ref, bf16[1024,512]{1,0:T(8,128)(2,1)} %convolution_convert_fusion.7.q_ref, bf16[2048,1024]{1,0:T(8,128)(2,1)} %convolution_convert_fusion.3.kv_ref, bf16[1024,512]{1,0:T(8,128)(2,1)} %get-tuple-element.38.o_ref, ...), custom_call_target="tpu_custom_call" | custom-call | tf_op jit(solution)/shard_map/attend_back/pallas_call | solution.py:380
  338.6 17.0 %attend_back.3 = (bf16[1024,512]{1,0:T(8,128)(2,1)}, bf16[2048,1024]{1,0:T(8,128)(2,1)}) custom-call(s32[4]{0:T(128)} %pad_add_fusion.info_ref, bf16[1024,512]{1,0:T(8,128)(2,1)} %convolution_convert_fusion.7.q_ref, bf16[2048,1024]{1,0:T(8,128)(2,1)} %convolution_convert_fusion.3.kv_ref, ...), custom_call_target="tpu_custom_call", output_to_operand_aliasing={{0}: (6, {}), {1}: (7, {})} | custom-call | tf_op jit(solution)/shard_map/attend_back/pallas_call | solution.py:380
  359.5 8.0 %fusion.19 = bf16[1024,1024]{1,0:T(8,128)(2,1)} fusion(bf16[2048,1024]{1,0:T(8,128)(2,1)S(1)} %copy-done.17, bf16[1024,1024]{0,1:T(8,128)(2,1)} %collective-permute-done.10, bf16[1024,1024]{0,1:T(8,128)(2,1)} %multiply_convert_fusion.1), kind=kOutput, calls=%fused_computation.58 | convolution fusion | flops 4304404480 | bytes 10485760 | tf_op jit(solution)/shard_map/dot_general | solution.py:26
  373.8 7.1 %fusion.63 = f32[2048,1024]{0,1:T(8,128)S(1)} fusion(bf16[2048,1024]{1,0:T(8,128)(2,1)} %get-tuple-element.48, bf16[1024,1024]{1,0:T(8,128)(2,1)} %bitcast.138), kind=kOutput, calls=%fused_computation.177 | convolution fusion | flops 4294967296 | bytes 14680064 | tf_op jit(solution)/shard_map/dot_general | solution.py:26
  396.4 6.8 %collective-permute-done.48 = bf16[4,64,2048]{2,1,0:T(8,128)(2,1)} collective-permute-done((bf16[4,64,2048]{2,1,0:T(8,128)(2,1)}, bf16[4,64,2048]{2,1,0:T(8,128)(2,1)}, u32[]{:S(2)}, u32[]{:S(2)}) %collective-permute-start.48) | collective-permute-done | bytes 1048608 | tf_op jit(solution)/shard_map/ppermute | solution.py:66
  413.1 5.8 %pick.5 = (bf16[8,64,2560]{2,1,0:T(8,128)(2,1)}, bf16[8,64,2560]{2,1,0:T(8,128)(2,1)}) custom-call(s32[16]{0:T(128)} %xor_bitcast_fusion.where_ref, bf16[16,64,512]{2,1,0:T(8,128)(2,1)} %bitcast.116, bf16[16,64,2048]{2,1,0:T(8,128)(2,1)} %bitcast.108), custom_call_target="tpu_custom_call" | custom-call | tf_op jit(solution)/shard_map/pick/pallas_call | solution.py:170
  418.9 6.3 %collective-permute-start.35 = (bf16[8,64,2560]{2,1,0:T(8,128)(2,1)}, bf16[8,64,2560]{2,1,0:T(8,128)(2,1)}, u32[]{:S(2)}, u32[]{:S(2)}) collective-permute-start(bf16[8,64,2560]{2,1,0:T(8,128)(2,1)} %get-tuple-element.51), channel_id=1, source_target_pairs={{0,2},{1,5},{2,0},{3,7},{4,6},{5,1},{6,4},{7,3},{8,10},{9,13},{10,... | collective-permute-start | bytes 7864328 | tf_op jit(solution)/shard_map/ppermute | solution.py:66
  425.3 7.1 %collective-permute-done.50 = bf16[1,64,2048]{2,1,0:T(8,128)(2,1)S(1)} collective-permute-done((bf16[1,64,2048]{2,1,0:T(8,128)(2,1)S(1)}, bf16[1,64,2048]{2,1,0:T(8,128)(2,1)S(1)}, u32[]{:S(2)}, u32[]{:S(2)}) %collective-permute-start.50) | collective-permute-done | bytes 262176 | tf_op jit(solution)/shard_map/ppermute | solution.py:66
  442.1 5.7 fusion.57
  450.9 7.9 %collective-permute-done.31 = bf16[4,64,1536]{2,1,0:T(8,128)(2,1)} collective-permute-done((bf16[4,64,1536]{2,1,0:T(8,128)(2,1)}, bf16[4,64,1536]{2,1,0:T(8,128)(2,1)}, u32[]{:S(2)}, u32[]{:S(2)}) %collective-permute-start.31) | collective-permute-done | bytes 786464 | tf_op jit(solution)/shard_map/ppermute | solution.py:66
  464.3 5.5 convolution_convert_fusion
  490.9 22.5 %collective-permute-done.41 = bf16[8,208,512]{2,1,0:T(8,128)(2,1)} collective-permute-done((bf16[8,208,512]{2,1,0:T(8,128)(2,1)}, bf16[8,208,512]{2,1,0:T(8,128)(2,1)}, u32[]{:S(2)}, u32[]{:S(2)}) %collective-permute-start.41) | collective-permute-done | bytes 1703968 | tf_op jit(solution)/shard_map/ppermute | solution.py:66
  532.3 5.7 %collective-permute-start.44 = (bf16[1,208,512]{2,1,0:T(8,128)(2,1)S(1)}, bf16[1,208,512]{2,1,0:T(8,128)(2,1)S(1)}, u32[]{:S(2)}, u32[]{:S(2)}) collective-permute-start(bf16[1,208,512]{2,1,0:T(8,128)(2,1)S(1)} %get-tuple-element.117), channel_id=1, source_target_pairs={{0,16},{1,17},{2,18},{3,19},{4,20},{5,21},{6,22},{7,23},{8,24},{9,... | collective-permute-start | bytes 638984 | tf_op jit(solution)/shard_map/ppermute | solution.py:66
  538.8 20.1 %collective-permute-done.38 = bf16[1,64,2560]{2,1,0:T(8,128)(2,1)S(1)} collective-permute-done((bf16[1,64,2560]{2,1,0:T(8,128)(2,1)S(1)}, bf16[1,64,2560]{2,1,0:T(8,128)(2,1)S(1)}, u32[]{:S(2)}, u32[]{:S(2)}) %collective-permute-start.38) | collective-permute-done | bytes 327712 | tf_op jit(solution)/shard_map/ppermute | solution.py:66
  (299 shorter events, 218.3 us)
Async XLA Ops:
  16.7 35.1 %collective-permute-start.4 = (bf16[1,64,3200]{2,1,0:T(8,128)(2,1)S(1)}, bf16[1,64,3200]{2,1,0:T(8,128)(2,1)S(1)}, u32[]{:S(2)}, u32[]{:S(2)}) collective-permute-start(bf16[1,64,3200]{2,1,0:T(8,128)(2,1)S(1)} %bitcast.120), channel_id=1, source_target_pairs={{0,16},{1,17},{2,18},{3,19},{4,20},{5,21},{6,22},{7,23},{8,24},{9,... | collective-permute-start | bytes 1228808 | tf_op jit(solution)/shard_map/ppermute | solution.py:66
  16.7 35.1 %collective-permute-start.3 = (bf16[1,64,3200]{2,1,0:T(8,128)(2,1)S(1)}, bf16[1,64,3200]{2,1,0:T(8,128)(2,1)S(1)}, u32[]{:S(2)}, u32[]{:S(2)}) collective-permute-start(bf16[1,64,3200]{2,1,0:T(8,128)(2,1)S(1)} %bitcast.121), channel_id=1, source_target_pairs={{0,8},{1,9},{2,10},{3,11},{4,12},{5,13},{6,14},{7,15},{8,0},{9,1},... | collective-permute-start | bytes 1228808 | tf_op jit(solution)/shard_map/ppermute | solution.py:66
  53.2 36.4 %collective-permute-start.6 = (bf16[4,64,3200]{2,1,0:T(8,128)(2,1)}, bf16[4,64,3200]{2,1,0:T(8,128)(2,1)}, u32[]{:S(2)}, u32[]{:S(2)}) collective-permute-start(bf16[4,64,3200]{2,1,0:T(8,128)(2,1)} %pad_maximum_fusion.11.refs_0_), channel_id=1, source_target_pairs={{0,4},{1,3},{2,6},{3,1},{4,0},{5,7},{6,2},{7,5},{8,12},{9,11},{10,... | collective-permute-start | bytes 4915208 | tf_op jit(solution)/shard_map/ppermute | solution.py:66
  56.4 45.7 %collective-permute-start = (bf16[256,3072]{1,0:T(8,128)(2,1)}, bf16[256,3072]{1,0:T(8,128)(2,1)}, u32[]{:S(2)}, u32[]{:S(2)}) collective-permute-start(bf16[256,3072]{1,0:T(8,128)(2,1)} %reshape_squeeze.4), channel_id=1, source_target_pairs={{0,1},{1,0},{2,3},{3,2},{4,5},{5,4},{6,7},{7,6},{8,9},{9,8},{10,11... | collective-permute-start | bytes 4718600 | tf_op jit(solution)/shard_map/ppermute | solution.py:75
  56.4 50.3 %collective-permute-start.7 = (bf16[4,64,3200]{2,1,0:T(8,128)(2,1)}, bf16[4,64,3200]{2,1,0:T(8,128)(2,1)}, u32[]{:S(2)}, u32[]{:S(2)}) collective-permute-start(bf16[4,64,3200]{2,1,0:T(8,128)(2,1)} %pad_maximum_fusion.11.refs_0_), channel_id=1, source_target_pairs={{0,2},{1,5},{2,0},{3,7},{4,6},{5,1},{6,4},{7,3},{8,10},{9,13},{10,... | collective-permute-start | bytes 4915208 | tf_op jit(solution)/shard_map/ppermute | solution.py:66
  89.6 21.4 %collective-permute-start.8 = (bf16[4,64,3200]{2,1,0:T(8,128)(2,1)}, bf16[4,64,3200]{2,1,0:T(8,128)(2,1)}, u32[]{:S(2)}, u32[]{:S(2)}) collective-permute-start(bf16[4,64,3200]{2,1,0:T(8,128)(2,1)} %collective-permute-done.6.refs_1_), channel_id=1, source_target_pairs={{0,2},{1,5},{2,0},{3,7},{4,6},{5,1},{6,4},{7,3},{8,10},{9,13},{10,... | collective-permute-start | bytes 4915208 | tf_op jit(solution)/shard_map/ppermute | solution.py:66
  92.1 31.8 %collective-permute-start.13 = (bf16[1,64,2560]{2,1,0:T(8,128)(2,1)S(1)}, bf16[1,64,2560]{2,1,0:T(8,128)(2,1)}, u32[]{:S(2)}, u32[]{:S(2)}) collective-permute-start(bf16[1,64,2560]{2,1,0:T(8,128)(2,1)S(1)} %maximum_bitcast_fusion), channel_id=1, source_target_pairs={{0,24},{1,25},{2,26},{3,27},{4,28},{5,29},{6,30},{7,31},{8,16},{9,... | collective-permute-start | bytes 983048 | tf_op jit(solution)/shard_map/ppermute | solution.py:66
  94.6 29.3 %collective-permute-start.12 = (bf16[1,64,2560]{2,1,0:T(8,128)(2,1)S(1)}, bf16[1,64,2560]{2,1,0:T(8,128)(2,1)}, u32[]{:S(2)}, u32[]{:S(2)}) collective-permute-start(bf16[1,64,2560]{2,1,0:T(8,128)(2,1)S(1)} %maximum_bitcast_fusion), channel_id=1, source_target_pairs={{0,16},{1,17},{2,18},{3,19},{4,20},{5,21},{6,22},{7,23},{8,24},{9,... | collective-permute-start | bytes 983048 | tf_op jit(solution)/shard_map/ppermute | solution.py:66
  102.1 21.8 %collective-permute-start.11 = (bf16[1,64,2560]{2,1,0:T(8,128)(2,1)S(1)}, bf16[1,64,2560]{2,1,0:T(8,128)(2,1)}, u32[]{:S(2)}, u32[]{:S(2)}) collective-permute-start(bf16[1,64,2560]{2,1,0:T(8,128)(2,1)S(1)} %maximum_bitcast_fusion), channel_id=1, source_target_pairs={{0,8},{1,9},{2,10},{3,11},{4,12},{5,13},{6,14},{7,15},{8,0},{9,1},... | collective-permute-start | bytes 983048 | tf_op jit(solution)/shard_map/ppermute | solution.py:66
  126.3 26.2 %collective-permute-start.14 = (bf16[4,64,2560]{2,1,0:T(8,128)(2,1)}, bf16[4,64,2560]{2,1,0:T(8,128)(2,1)}, u32[]{:S(2)}, u32[]{:S(2)}) collective-permute-start(bf16[4,64,2560]{2,1,0:T(8,128)(2,1)} %pad_maximum_fusion.22.refs_0_), channel_id=1, source_target_pairs={{0,4},{1,3},{2,6},{3,1},{4,0},{5,7},{6,2},{7,5},{8,12},{9,11},{10,... | collective-permute-start | bytes 3932168 | tf_op jit(solution)/shard_map/ppermute | solution.py:66
  133.7 57.0 %collective-permute-start.10 = (bf16[1024,1024]{0,1:T(8,128)(2,1)}, bf16[1024,1024]{0,1:T(8,128)(2,1)}, u32[]{:S(2)}, u32[]{:S(2)}) collective-permute-start(bf16[1024,1024]{0,1:T(8,128)(2,1)} %multiply_convert_fusion.1), channel_id=1, source_target_pairs={{0,1},{1,0},{2,3},{3,2},{4,5},{5,4},{6,7},{7,6},{8,9},{9,8},{10,11... | collective-permute-start | bytes 6291464 | tf_op jit(solution)/shard_map/ppermute | solution.py:75
  133.8 47.5 %collective-permute-start.15 = (bf16[4,64,2560]{2,1,0:T(8,128)(2,1)}, bf16[4,64,2560]{2,1,0:T(8,128)(2,1)S(1)}, u32[]{:S(2)}, u32[]{:S(2)}) collective-permute-start(bf16[4,64,2560]{2,1,0:T(8,128)(2,1)} %pad_maximum_fusion.22.refs_0_), channel_id=1, source_target_pairs={{0,2},{1,5},{2,0},{3,7},{4,6},{5,1},{6,4},{7,3},{8,10},{9,13},{10,... | collective-permute-start | bytes 3932168 | tf_op jit(solution)/shard_map/ppermute | solution.py:66
  152.5 28.8 %collective-permute-start.16 = (bf16[4,64,2560]{2,1,0:T(8,128)(2,1)}, bf16[4,64,2560]{2,1,0:T(8,128)(2,1)S(1)}, u32[]{:S(2)}, u32[]{:S(2)}) collective-permute-start(bf16[4,64,2560]{2,1,0:T(8,128)(2,1)} %collective-permute-done.14.refs_1_), channel_id=1, source_target_pairs={{0,2},{1,5},{2,0},{3,7},{4,6},{5,1},{6,4},{7,3},{8,10},{9,13},{10,... | collective-permute-start | bytes 3932168 | tf_op jit(solution)/shard_map/ppermute | solution.py:66
  181.0 49.2 %collective-permute-start.22 = (bf16[4,64,2048]{2,1,0:T(8,128)(2,1)}, bf16[4,64,2048]{2,1,0:T(8,128)(2,1)}, u32[]{:S(2)}, u32[]{:S(2)}) collective-permute-start(bf16[4,64,2048]{2,1,0:T(8,128)(2,1)} %pad_maximum_fusion.23.refs_0_), channel_id=1, source_target_pairs={{0,4},{1,3},{2,6},{3,1},{4,0},{5,7},{6,2},{7,5},{8,12},{9,11},{10,... | collective-permute-start | bytes 3145736 | tf_op jit(solution)/shard_map/ppermute | solution.py:66
  230.2 26.0 %collective-permute-start.24 = (bf16[4,64,2048]{2,1,0:T(8,128)(2,1)}, bf16[4,64,2048]{2,1,0:T(8,128)(2,1)}, u32[]{:S(2)}, u32[]{:S(2)}) collective-permute-start(bf16[4,64,2048]{2,1,0:T(8,128)(2,1)} %collective-permute-done.22.refs_1_), channel_id=1, source_target_pairs={{0,2},{1,5},{2,0},{3,7},{4,6},{5,1},{6,4},{7,3},{8,10},{9,13},{10,... | collective-permute-start | bytes 3145736 | tf_op jit(solution)/shard_map/ppermute | solution.py:66
  237.3 24.0 %collective-permute-start.18 = (bf16[512,1024]{0,1:T(8,128)(2,1)}, bf16[512,1024]{0,1:T(8,128)(2,1)}, u32[]{:S(2)}, u32[]{:S(2)}) collective-permute-start(bf16[512,1024]{0,1:T(8,128)(2,1)} %multiply_convert_fusion.2), channel_id=1, source_target_pairs={{0,1},{1,0},{2,3},{3,2},{4,5},{5,4},{6,7},{7,6},{8,9},{9,8},{10,11... | collective-permute-start | bytes 3145736 | tf_op jit(solution)/shard_map/ppermute | solution.py:75
  239.1 31.8 %collective-permute-start.26 = (bf16[512,1024]{0,1:T(8,128)(2,1)S(1)}, bf16[512,1024]{0,1:T(8,128)(2,1)}, u32[]{:S(2)}, u32[]{:S(2)}) collective-permute-start(bf16[512,1024]{0,1:T(8,128)(2,1)S(1)} %bitcast.105), channel_id=1, source_target_pairs={{0,1},{1,0},{2,3},{3,2},{4,5},{5,4},{6,7},{7,6},{8,9},{9,8},{10,11... | collective-permute-start | bytes 3145736 | tf_op jit(solution)/shard_map/ppermute | solution.py:75
  295.8 22.5 %collective-permute-start.28 = (bf16[512,1024]{0,1:T(8,128)(2,1)}, bf16[512,1024]{0,1:T(8,128)(2,1)S(1)}, u32[]{:S(2)}, u32[]{:S(2)}) collective-permute-start(bf16[512,1024]{0,1:T(8,128)(2,1)} %fusion.56), channel_id=1, source_target_pairs={{0,1},{1,0},{2,3},{3,2},{4,5},{5,4},{6,7},{7,6},{8,9},{9,8},{10,11... | collective-permute-start | bytes 3145736 | tf_op jit(solution)/shard_map/ppermute | solution.py:75
  308.5 72.5 %collective-permute-start.47 = (bf16[8,64,2048]{2,1,0:T(8,128)(2,1)}, bf16[8,64,2048]{2,1,0:T(8,128)(2,1)S(1)}, u32[]{:S(2)}, u32[]{:S(2)}) collective-permute-start(bf16[8,64,2048]{2,1,0:T(8,128)(2,1)} %get-tuple-element.55), channel_id=1, source_target_pairs={{0,2},{1,5},{2,0},{3,7},{4,6},{5,1},{6,4},{7,3},{8,10},{9,13},{10,... | collective-permute-start | bytes 6291464 | tf_op jit(solution)/shard_map/ppermute | solution.py:66
  372.0 62.5 %collective-permute-start.30 = (bf16[8,64,1536]{2,1,0:T(8,128)(2,1)}, bf16[8,64,1536]{2,1,0:T(8,128)(2,1)}, u32[]{:S(2)}, u32[]{:S(2)}) collective-permute-start(bf16[8,64,1536]{2,1,0:T(8,128)(2,1)} %get-tuple-element.47), channel_id=1, source_target_pairs={{0,2},{1,5},{2,0},{3,7},{4,6},{5,1},{6,4},{7,3},{8,10},{9,13},{10,... | collective-permute-start | bytes 4718600 | tf_op jit(solution)/shard_map/ppermute | solution.py:66
  389.3 48.8 %collective-permute-start.29 = (bf16[1024,1024]{0,1:T(8,128)(2,1)}, bf16[1024,1024]{0,1:T(8,128)(2,1)}, u32[]{:S(2)}, u32[]{:S(2)}) collective-permute-start(bf16[1024,1024]{0,1:T(8,128)(2,1)} %pad_maximum_fusion.8), channel_id=1, source_target_pairs={{0,1},{1,0},{2,3},{3,2},{4,5},{5,4},{6,7},{7,6},{8,9},{9,8},{10,11... | collective-permute-start | bytes 6291464 | tf_op jit(solution)/shard_map/ppermute | solution.py:75
  409.2 23.2 %collective-permute-start.50 = (bf16[1,64,2048]{2,1,0:T(8,128)(2,1)S(1)}, bf16[1,64,2048]{2,1,0:T(8,128)(2,1)S(1)}, u32[]{:S(2)}, u32[]{:S(2)}) collective-permute-start(bf16[1,64,2048]{2,1,0:T(8,128)(2,1)S(1)} %get-tuple-element.112), channel_id=1, source_target_pairs={{0,16},{1,17},{2,18},{3,19},{4,20},{5,21},{6,22},{7,23},{8,24},{9,... | collective-permute-start | bytes 786440 | tf_op jit(solution)/shard_map/ppermute | solution.py:66
  418.9 60.3 %collective-permute-start.35 = (bf16[8,64,2560]{2,1,0:T(8,128)(2,1)}, bf16[8,64,2560]{2,1,0:T(8,128)(2,1)}, u32[]{:S(2)}, u32[]{:S(2)}) collective-permute-start(bf16[8,64,2560]{2,1,0:T(8,128)(2,1)} %get-tuple-element.51), channel_id=1, source_target_pairs={{0,2},{1,5},{2,0},{3,7},{4,6},{5,1},{6,4},{7,3},{8,10},{9,13},{10,... | collective-permute-start | bytes 7864328 | tf_op jit(solution)/shard_map/ppermute | solution.py:66
  460.8 28.7 %collective-permute-start.32 = (bf16[1,64,1536]{2,1,0:T(8,128)(2,1)}, bf16[1,64,1536]{2,1,0:T(8,128)(2,1)}, u32[]{:S(2)}, u32[]{:S(2)}) collective-permute-start(bf16[1,64,1536]{2,1,0:T(8,128)(2,1)} %get-tuple-element.118), channel_id=1, source_target_pairs={{0,8},{1,9},{2,10},{3,11},{4,12},{5,13},{6,14},{7,15},{8,0},{9,1},... | collective-permute-start | bytes 589832 | tf_op jit(solution)/shard_map/ppermute | solution.py:66
  460.8 28.7 %collective-permute-start.34 = (bf16[1,64,1536]{2,1,0:T(8,128)(2,1)}, bf16[1,64,1536]{2,1,0:T(8,128)(2,1)}, u32[]{:S(2)}, u32[]{:S(2)}) collective-permute-start(bf16[1,64,1536]{2,1,0:T(8,128)(2,1)} %get-tuple-element.119), channel_id=1, source_target_pairs={{0,24},{1,25},{2,26},{3,27},{4,28},{5,29},{6,30},{7,31},{8,16},{9,... | collective-permute-start | bytes 589832 | tf_op jit(solution)/shard_map/ppermute | solution.py:66
  461.8 27.7 %collective-permute-start.33 = (bf16[1,64,1536]{2,1,0:T(8,128)(2,1)}, bf16[1,64,1536]{2,1,0:T(8,128)(2,1)}, u32[]{:S(2)}, u32[]{:S(2)}) collective-permute-start(bf16[1,64,1536]{2,1,0:T(8,128)(2,1)} %get-tuple-element.120), channel_id=1, source_target_pairs={{0,16},{1,17},{2,18},{3,19},{4,20},{5,21},{6,22},{7,23},{8,24},{9,... | collective-permute-start | bytes 589832 | tf_op jit(solution)/shard_map/ppermute | solution.py:66
  474.6 38.8 %collective-permute-start.41 = (bf16[8,208,512]{2,1,0:T(8,128)(2,1)}, bf16[8,208,512]{2,1,0:T(8,128)(2,1)}, u32[]{:S(2)}, u32[]{:S(2)}) collective-permute-start(bf16[8,208,512]{2,1,0:T(8,128)(2,1)} %get-tuple-element.53), channel_id=1, source_target_pairs={{0,2},{1,5},{2,0},{3,7},{4,6},{5,1},{6,4},{7,3},{8,10},{9,13},{10,... | collective-permute-start | bytes 5111816 | tf_op jit(solution)/shard_map/ppermute | solution.py:66
  483.8 34.5 %collective-permute-start.36 = (bf16[4,64,2560]{2,1,0:T(8,128)(2,1)}, bf16[4,64,2560]{2,1,0:T(8,128)(2,1)}, u32[]{:S(2)}, u32[]{:S(2)}) collective-permute-start(bf16[4,64,2560]{2,1,0:T(8,128)(2,1)} %get-tuple-element.98), channel_id=1, source_target_pairs={{0,4},{1,3},{2,6},{3,1},{4,0},{5,7},{6,2},{7,5},{8,12},{9,11},{10,... | collective-permute-start | bytes 3932168 | tf_op jit(solution)/shard_map/ppermute | solution.py:66
  523.2 35.7 %collective-permute-start.38 = (bf16[1,64,2560]{2,1,0:T(8,128)(2,1)S(1)}, bf16[1,64,2560]{2,1,0:T(8,128)(2,1)S(1)}, u32[]{:S(2)}, u32[]{:S(2)}) collective-permute-start(bf16[1,64,2560]{2,1,0:T(8,128)(2,1)S(1)} %get-tuple-element.108), channel_id=1, source_target_pairs={{0,16},{1,17},{2,18},{3,19},{4,20},{5,21},{6,22},{7,23},{8,24},{9,... | collective-permute-start | bytes 983048 | tf_op jit(solution)/shard_map/ppermute | solution.py:66
  528.8 32.1 %collective-permute-start.43 = (bf16[1,208,512]{2,1,0:T(8,128)(2,1)S(1)}, bf16[1,208,512]{2,1,0:T(8,128)(2,1)S(1)}, u32[]{:S(2)}, u32[]{:S(2)}) collective-permute-start(bf16[1,208,512]{2,1,0:T(8,128)(2,1)S(1)} %get-tuple-element.115), channel_id=1, source_target_pairs={{0,8},{1,9},{2,10},{3,11},{4,12},{5,13},{6,14},{7,15},{8,0},{9,1},... | collective-permute-start | bytes 638984 | tf_op jit(solution)/shard_map/ppermute | solution.py:66
  529.6 31.3 %collective-permute-start.45 = (bf16[1,208,512]{2,1,0:T(8,128)(2,1)S(1)}, bf16[1,208,512]{2,1,0:T(8,128)(2,1)S(1)}, u32[]{:S(2)}, u32[]{:S(2)}) collective-permute-start(bf16[1,208,512]{2,1,0:T(8,128)(2,1)S(1)} %get-tuple-element.116), channel_id=1, source_target_pairs={{0,24},{1,25},{2,26},{3,27},{4,28},{5,29},{6,30},{7,31},{8,16},{9,... | collective-permute-start | bytes 638984 | tf_op jit(solution)/shard_map/ppermute | solution.py:66
  532.3 33.1 %collective-permute-start.44 = (bf16[1,208,512]{2,1,0:T(8,128)(2,1)S(1)}, bf16[1,208,512]{2,1,0:T(8,128)(2,1)S(1)}, u32[]{:S(2)}, u32[]{:S(2)}) collective-permute-start(bf16[1,208,512]{2,1,0:T(8,128)(2,1)S(1)} %get-tuple-element.117), channel_id=1, source_target_pairs={{0,16},{1,17},{2,18},{3,19},{4,20},{5,21},{6,22},{7,23},{8,24},{9,... | collective-permute-start | bytes 638984 | tf_op jit(solution)/shard_map/ppermute | solution.py:66
  (72 other events, 993.9 us)
